TPU v7x, 256 devices: a whole 4x4x8 slice. The times are simulated.
256 devices in a mesh: seq: 32 (over z, y), chan: 8 (over x, core).
Axes of the slice: x: 4, y: 4, z: 8, core: 2. Of those that a mesh axis runs over, the one named last changes fastest.
Arguments:
- hyena_query: bfloat16 [4096, 8192], P('chan', 'seq'), may hold values from -36 to 36
- hyena_key: bfloat16 [4096, 8192], P('chan', 'seq'), may hold values from -6 to 6
- hyena_value: bfloat16 [4096, 8192], P('chan', 'seq'), may hold values from -6 to 6
- long_filter: float32 [4096, 8192], P(('chan', 'seq')), may hold values from -4 to 4
- skip_weight: float32 [4096], P(('chan', 'seq')), may hold values from 0.5 to 1.5
- stripe_order: int32 [8192], replicated, may hold values from 0 to 8191, as said below
- query_rows: bfloat16 [8192, 4096], P('seq', 'chan'), may hold values from -6 to 6
- key_rows: bfloat16 [8192, 4096], P('seq', 'chan'), may hold values from -6 to 6
- norm_gain: float32 [4096], P('chan'), may hold values from 0.1 to 1.9
Outputs:
- hyena_output: bfloat16 [4096, 8192], P('chan', 'seq')
- attended: bfloat16 [8192, 4096], P('seq', 'chan')
Inputs may be any that keep to these rules, and one draw needn't show every extreme that they name: stripe_order[256 * s + j] = 32 * j + sigma(s) for 0 <= j < 256 and 0 <= s < 32, where sigma is a permutation of 0 to 31.
All inputs are finite; a program needn't handle non-finite values.
Results may differ from a plain program's by a relative error of at most 0.012.
Values may be sent and summed in bfloat16 or wider, within the bound.
No kernel may reach another device: no remote copies, remote signals or barrier semaphores. Data moves between devices by JAX's collectives and lax.ppermute only.
A program may use at most 128 MiB of HBM per device.

v0:
```python
import functools
import math

import jax
import jax.numpy as jnp
import numpy as np
from jax import lax
from jax.experimental import pallas as pl
from jax.experimental.pallas import tpu as pltpu
from jax.sharding import PartitionSpec as P


D = 4096
HEAD_DIM = 128
EPS = 1e-05
BF = jnp.bfloat16
F32 = jnp.float32
VMEM = pl.BlockSpec(memory_space=pltpu.VMEM)
SMEM = pl.BlockSpec(memory_space=pltpu.SMEM)
ANY = pl.BlockSpec(memory_space=pl.ANY)
HBM = pl.BlockSpec(memory_space=pltpu.HBM)


def split_np(table):
    hi = table.astype(np.float32).astype(BF)
    lo = (table - hi.astype(np.float64)).astype(np.float32).astype(BF)
    return hi, lo


def transform_tables():
    k1 = np.arange(32)[:, None] + 0.25
    a = np.arange(32)[None, :]
    b = np.arange(256)[None, :]
    first = 2.0 * np.pi * k1 * a / 32.0
    twist = 2.0 * np.pi * k1 * b / 8192.0
    inner = 2.0 * np.pi * ((np.arange(256)[:, None] * b) % 256) / 256.0
    f1 = np.concatenate([np.cos(first), -np.sin(first)], axis=0)
    f1hi, f1lo = split_np(f1)
    f2 = np.concatenate([np.cos(first).T, -np.sin(first).T], axis=1)
    f2hi, f2lo = split_np(f2)
    chi, clo = split_np(np.cos(inner))
    shi, slo = split_np(np.sin(inner))
    return dict(
        f1=np.concatenate([f1hi, f1lo], axis=0),
        f2=np.concatenate([f2hi, f2lo], axis=0),
        tc=np.cos(twist).astype(np.float32),
        ts=np.sin(twist).astype(np.float32),
        w=np.stack([chi, clo, shi, slo]),
    )


def split(x):
    hi = x.astype(BF)
    lo = (x - hi.astype(F32)).astype(BF)
    return hi, lo


def dot(x, w):
    return jnp.dot(x, w, preferred_element_type=F32)


def dot3(x, w_hi, w_lo):
    hi, lo = x
    return dot(hi, w_hi) + (dot(hi, w_lo) + dot(lo, w_hi))


def pack_kernel(hk, hv, hq, q, k, out, vk, vv, vq, wq, wk, scr, sem):
    copies = []
    for n, (src, dst) in enumerate(((q, wq), (k, wk), (hk, vk), (hv, vv), (hq, vq))):
        rows = src.shape[0] // 2
        for half in range(2):
            part = pl.ds(half * rows, rows)
            copies.append(pltpu.make_async_copy(src.at[part], dst.at[part], sem.at[2 * n + half]))
    for c in copies:
        c.start()
    for c in copies[:4]:
        c.wait()
    for h in range(4):
        cols = slice(h * 128, h * 128 + 128)
        scr[h] = wq[:, cols].astype(F32)
        for i in range(8):
            d = h * 8 + i
            out[d, 64:96, :] = scr[h, pl.ds(i, 32, stride=8), :].astype(BF)
            out[d, 96:128, :] = wk[i * 32 : i * 32 + 32, cols]
    for c in copies[4:]:
        c.wait()
    prod = (vk[...].astype(F32) * vv[...].astype(F32)).astype(BF)
    for half in range(2):
        lanes = slice(half * 128, half * 128 + 128)
        rows = slice(half * 16, half * 16 + 16)
        out[:, rows, :] = prod[:, lanes].reshape(32, 16, 128)
        out[:, half * 16 + 32 : half * 16 + 48, :] = vq[:, lanes].reshape(32, 16, 128)


def filter_kernel(h, f1h, f2h, tch, tsh, wh, hr, hi, f1, f2, tc, ts, w, br, bi, sem):
    copies = [
        pltpu.make_async_copy(src, dst, sem.at[n])
        for n, (src, dst) in enumerate(((f1h, f1), (f2h, f2), (tch, tc), (tsh, ts), (wh, w)))
    ]
    for copy in copies:
        copy.start()
    for copy in copies:
        copy.wait()
    for c in range(16):
        xh, xl = split(h[c])
        wide = dot(f1[...], xh)
        a = wide[:64] + wide[64:] + dot(f1[:64, :], xl)
        ar, ai = a[:32], a[32:]
        br[c * 32 : c * 32 + 32, :] = ar * tc[...] + ai * ts[...]
        bi[c * 32 : c * 32 + 32, :] = ai * tc[...] - ar * ts[...]
    rr = split(br[...])
    ii = split(bi[...])
    norm = 1.0 / 8192.0
    hr[...] = (dot3(rr, w[0], w[1]) + dot3(ii, w[2], w[3])) * norm
    hi[...] = (dot3(ii, w[0], w[1]) - dot3(rr, w[2], w[3])) * norm


def conv_kernel(info, x, skip, hr, hi, f1, f2, tc, ts, wh, out, xs, qs, br, bi, w, sem):
    table = pltpu.make_async_copy(wh, w, sem)
    table.start()
    for half in range(2):
        xs[half] = x[:, half * 16 : half * 16 + 16, :].reshape(512, 128).astype(F32)
        qs[half] = x[:, half * 16 + 32 : half * 16 + 48, :].reshape(512, 128).astype(F32)

    def channel(ref, c):
        rows = pl.ds(c, 32, stride=16)
        return jnp.concatenate([ref[0, rows, :], ref[1, rows, :]], axis=1)

    for c in range(16):
        wide = dot(f1[...], channel(xs, c).astype(BF))
        a = wide[:64] + wide[64:]
        ar, ai = a[:32], a[32:]
        br[c * 32 : c * 32 + 32, :] = ar * tc[...] + ai * ts[...]
        bi[c * 32 : c * 32 + 32, :] = ai * tc[...] - ar * ts[...]
    table.wait()
    rr = split(br[...])
    ii = split(bi[...])
    xr = dot3(rr, w[0], w[1]) + dot3(ii, w[2], w[3])
    xi = dot3(ii, w[0], w[1]) - dot3(rr, w[2], w[3])
    yr = split(xr * hr[...] - xi * hi[...])
    yi = split(xr * hi[...] + xi * hr[...])
    br[...] = dot3(yr, w[0], w[1]) - dot3(yi, w[2], w[3])
    bi[...] = dot3(yr, w[2], w[3]) + dot3(yi, w[0], w[1])
    for c in range(16):
        gr = br[c * 32 : c * 32 + 32, :]
        gi = bi[c * 32 : c * 32 + 32, :]
        d = jnp.concatenate([gr * tc[...] - gi * ts[...], gr * ts[...] + gi * tc[...]], axis=0)
        dh, dl = split(d)
        wide = dot(f2[...], dh)
        y = wide[:32] + wide[32:] + dot(f2[:32, :], dl)
        rows = pl.ds(c, 32, stride=16)
        g = (channel(qs, c) * (y + skip[c] * channel(xs, c))).astype(BF).astype(F32)
        qs[0, rows, :] = g[:, :128]
        qs[1, rows, :] = g[:, 128:]
    for half in range(2):
        lanes = slice(half * 128, half * 128 + 128)
        out[:, :, lanes] = qs[half].astype(BF).reshape(32, 16, 128)


def order_kernel(info, x, kout, qout, ks, qs):
    for r in range(32):
        ks[pl.ds(r, 32, stride=32), :] = x[info[32 + r], 96:128, :].astype(F32)
    kout[...] = ks[...].astype(BF)
    for s in range(32):
        qs[pl.ds(s, 32, stride=32), :] = x[s, 64:96, :].astype(F32)
    qout[...] = qs[...].astype(BF)


def keys_kernel(info, *rest):
    shards, (out, sem) = rest[:8], rest[8:]
    copies = [
        pltpu.make_async_copy(shards[n], out.at[info[64 + n]], sem.at[n]) for n in range(8)
    ]
    for c in copies:
        c.start()
    for c in copies:
        c.wait()


NT = (((1,), (1,)), ((), ()))
PIECES = ((7, 7), (6, 6), (4, 5), (0, 3))


def score_kernel(tiles, qloc, q, keys, p, total, s, peak):
    first, last = tiles
    scale = math.log2(math.e) / math.sqrt(HEAD_DIM)
    for tile in range(first, last + 1):
        base = (tile - first) * 128
        query = q[tile * 128 : tile * 128 + 128, :]

        def scores(chunk, quarter):
            kb = keys[chunk, quarter * 256 : quarter * 256 + 256, :]
            return lax.dot_general(query, kb, NT, preferred_element_type=F32)

        def columns(chunk, quarter):
            return pl.ds(pl.multiple_of(chunk * 1024 + quarter * 256, 256), 256)

        def plain(chunk, top):
            for quarter in range(4):
                v = scores(chunk, quarter)
                s[:, columns(chunk, quarter)] = v
                top = jnp.maximum(top, v)
            return top

        top = jnp.full((128, 256), -1e30, F32)
        top = lax.fori_loop(0, tile, plain, top)
        peak[...] = top
        for quarter in range(4):
            low = quarter * 32
            kb = keys[tile, quarter * 256 : quarter * 256 + 256, :]
            v = lax.dot_general(query[low:], kb, NT, preferred_element_type=F32)
            place = lax.broadcasted_iota(jnp.int32, (128 - low, 256), 1) + quarter * 256
            v = jnp.where(place <= qloc[low:, :], v, -1e30)
            start = tile * 1024 + quarter * 256
            s[low:, start : start + 256] = v
            peak[low:, :] = jnp.maximum(peak[low:, :], v)
        top = peak[...]
        top = jnp.max(top, axis=1, keepdims=True)

        def weigh(chunk, acc):
            for quarter in range(4):
                cols = columns(chunk, quarter)
                e = jnp.exp2((s[:, cols] - top) * scale)
                p[base : base + 128, cols] = e.astype(BF)
                acc = acc + e
            return acc

        peak[...] = lax.fori_loop(0, tile, weigh, jnp.zeros((128, 256), F32))
        for quarter in range(4):
            low = quarter * 32
            start = tile * 1024 + quarter * 256
            e = jnp.exp2((s[low:, start : start + 256] - top[low:, :]) * scale)
            p[base + low : base + 128, start : start + 256] = e.astype(BF)
            if low:
                p[base : base + low, start : start + 256] = jnp.zeros((low, 256), BF)
            peak[low:, :] += e
        total[base : base + 128, :] = jnp.sum(peak[...], axis=1, keepdims=True)


def vals_kernel(info, *rest):
    shards, (vals, hyena, ss, hs, sem) = rest[:8], rest[8:]
    copies = [
        pltpu.make_async_copy(
            shards[n], vals.at[:, pl.ds(pl.multiple_of(info[64 + n] * 16, 16), 16), :], sem.at[n]
        )
        for n in range(8)
    ]
    for c in copies:
        c.start()
    for c in copies:
        c.wait()
    for a in range(32):
        wide = vals[a].astype(F32)
        ss[a : a + 1, :] = jnp.sum(wide * wide, axis=0, keepdims=True)
    own = info[64]
    for n in range(4):
        hs[n * 256 : n * 256 + 256, :] = vals[own * 4 + n].astype(F32).T
    for st in range(32):
        hyena[st] = hs[pl.ds(info[st], 32, stride=32), :].astype(BF)


def value_kernel(ss, gain, vals, hyena, *rest):
    ps, totals, (back, norm, acc, rows) = rest[:4], rest[4:8], rest[8:]
    inv = lax.rsqrt(ss[...] * (1.0 / D) + EPS)
    wide = jnp.broadcast_to(gain[...], (128, 128)).T
    wide = jnp.concatenate([wide, wide], axis=1)
    for a in range(32):
        scaled = vals[a].astype(F32) * inv[a : a + 1, :] * wide
        norm[:, a * 256 : a * 256 + 256] = scaled.astype(BF)

    def product(p, low, start, width):
        return lax.dot_general(
            p[low:, start : start + width],
            norm[:, start : start + width],
            NT,
            preferred_element_type=F32,
        )

    for (first, last), p, total in zip(PIECES, ps, totals):
        end = (last + 1) * 128
        acc[first * 128 : end, :] = product(p, 0, 0, first * 1024 + 256)
        for n in range(first * 4 + 1, (last + 1) * 4):
            acc[n * 32 : end, :] += product(p, n * 32 - first * 128, n * 256, 256)
        for tile in range(first, last + 1):
            base = (tile - first) * 128
            o = acc[tile * 128 : tile * 128 + 128, :] / total[base : base + 128, :]
            for n in range(4):
                rows[pl.ds(tile * 4 + n, 32, stride=32), :] = o[n * 32 : n * 32 + 32, :]
    back[:, 0:32, :] = rows[...].astype(BF).reshape(32, 32, 128)
    back[:, 32:64, :] = hyena[...]


def unpack_kernel(x, banded, att, scr, bs):
    for h in range(4):
        for i in range(8):
            scr[pl.ds(i, 32, stride=8), :] = x[h * 8 + i, 0:32, :].astype(F32)
            bs[i * 32 : i * 32 + 32, :] = x[h * 8 + i, 32:64, :].astype(F32)
        banded[h * 128 : h * 128 + 128, :] = bs[...].T.astype(BF)
        att[:, h * 128 : h * 128 + 128] = scr[...].astype(BF)


def ring(step):
    return [(n, (n // 4) * 4 + (n % 4 + step) % 4) for n in range(32)]


ACROSS = [(n, n ^ 4) for n in range(32)]


def block_gather(tag, own):
    up, down = ring(1), ring(-1)
    left = lax.ppermute(own, "seq", up)
    right = lax.ppermute(own, "seq", down)
    other = lax.ppermute(own, "seq", ACROSS)
    far = lax.ppermute(left, "seq", up)
    other_left = lax.ppermute(left, "seq", ACROSS)
    other_right = lax.ppermute(other, "seq", down)
    if tag == "k":
        other_far = lax.ppermute(other_left, "seq", up)
    else:
        other_far = lax.ppermute(other_right, "seq", down)
    return [own, left, right, far, other, other_left, other_right, other_far]


def all_sum(x):
    for axis, flips in (("chan", (1,)), ("chan", (2, 4, 6)), ("seq", (8, 16, 24))):
        size = 8 if axis == "chan" else 32
        parts = [lax.ppermute(x, axis, [(d, d ^ f) for d in range(size)]) for f in flips]
        for part in parts:
            x = x + part
    return x


LIMITS = dict(pack=8, filter=12, order=6, conv=14, keys=2, vals=4, value=12, unpack=6)


def kernel(body, label, **keywords):
    limit = LIMITS.get(label, 12)
    return pl.pallas_call(body, compiler_params=params(limit), **keywords)


def params(mib=48):
    return pltpu.CompilerParams(vmem_limit_bytes=mib << 20)


def in_hbm(x):
    return pltpu.with_memory_space_constraint(x, pltpu.HBM)


def shape(dims, dtype):
    return jax.ShapeDtypeStruct(dims, dtype)


def local(
    hyena_query,
    hyena_key,
    hyena_value,
    long_filter,
    skip_weight,
    stripe_order,
    query_rows,
    key_rows,
    norm_gain,
):
    t = {name: jnp.asarray(v) for name, v in transform_tables().items()}
    sigma = stripe_order.reshape(32, 256)[:, 0]
    numbers = jnp.arange(32, dtype=jnp.int32)
    sinv = jnp.sum(jnp.where(sigma[:, None] == numbers[None, :], numbers[:, None], 0), axis=0)
    seq = lax.axis_index("seq")
    head, inner = seq // 8, seq % 8
    y, z = inner % 4, inner // 4
    near, far_side = z * 4, (1 - z) * 4
    slots = [near + y, near + (y + 3) % 4, near + (y + 1) % 4, near + (y + 2) % 4]
    slots += [far_side + y, far_side + (y + 3) % 4, far_side + (y + 1) % 4]
    slots += [far_side + (y + 2) % 4]
    info = jnp.concatenate([sigma, sinv, jnp.stack(slots)]).astype(jnp.int32)
    row = jnp.arange(128, dtype=jnp.int32)
    qloc = (256 * (row // 32) + 32 * inner + jnp.tile(sigma, 4))[:, None]

    packed = kernel(
        pack_kernel,
        "pack",
        out_shape=shape((32, 128, 128), BF),
        in_specs=[HBM] * 5,
        out_specs=VMEM,
        scratch_shapes=[pltpu.VMEM((512, 256), BF)] * 3
        + [pltpu.VMEM((256, 512), BF)] * 2
        + [pltpu.VMEM((4, 256, 128), F32), pltpu.SemaphoreType.DMA((10,))],
    )(*(in_hbm(x) for x in (hyena_key, hyena_value, hyena_query, query_rows, key_rows)))
    spread = lax.all_to_all(packed, "seq", 0, 0, tiled=True)

    gain = lax.dynamic_slice_in_dim(norm_gain, head * 128, 128)[None, :]
    long_filter, info, qloc, gain = lax.optimization_barrier(
        (long_filter.reshape(16, 32, 256), info, qloc, gain)
    )
    hr, hi, f1, f2, tc, ts = kernel(
        filter_kernel,
        "filter",
        out_shape=(shape((512, 256), F32), shape((512, 256), F32))
        + tuple(shape(t[n].shape, t[n].dtype) for n in ("f1", "f2", "tc", "ts")),
        in_specs=[VMEM] + [HBM] * 5,
        out_specs=(VMEM,) * 6,
        scratch_shapes=[pltpu.VMEM((4, 256, 256), BF)]
        + [pltpu.VMEM((512, 256), F32)] * 2
        + [pltpu.SemaphoreType.DMA((5,))],
    )(long_filter, *(in_hbm(t[n]) for n in ("f1", "f2", "tc", "ts", "w")))
    spread, hr = lax.optimization_barrier((spread, hr))

    kn, qn = kernel(
        order_kernel,
        "order",
        out_shape=(shape((1024, 128), BF), shape((1024, 128), BF)),
        in_specs=[SMEM, VMEM],
        out_specs=(VMEM, VMEM),
        scratch_shapes=[pltpu.VMEM((1024, 128), F32)] * 2,
    )(info, spread)
    key_shards = block_gather("k", kn)

    gated = kernel(
        conv_kernel,
        "conv",
        out_shape=shape((32, 16, 256), BF),
        in_specs=[SMEM, VMEM, SMEM] + [VMEM] * 6 + [HBM],
        out_specs=VMEM,
        scratch_shapes=[pltpu.VMEM((2, 512, 128), F32)] * 2
        + [pltpu.VMEM((512, 256), F32)] * 2
        + [pltpu.VMEM((4, 256, 256), BF), pltpu.SemaphoreType.DMA],
    )(info, spread, skip_weight, hr, hi, f1, f2, tc, ts, in_hbm(t["w"]))
    value_shards = block_gather("v", gated)

    keys = kernel(
        keys_kernel,
        "keys",
        out_shape=shape((8, 1024, 128), BF),
        in_specs=[SMEM] + [ANY] * 8,
        out_specs=VMEM,
        scratch_shapes=[pltpu.SemaphoreType.DMA((8,))],
    )(info, *key_shards)
    ps, totals = [], []
    for n, tiles in enumerate(PIECES):
        count = (tiles[1] - tiles[0] + 1) * 128
        width = (tiles[1] + 1) * 1024
        p, total = kernel(
            functools.partial(score_kernel, tiles),
            "score%d" % n,
            out_shape=(shape((count, width), BF), shape((count, 1), F32)),
            in_specs=[VMEM] * 3,
            out_specs=(VMEM, VMEM),
            scratch_shapes=[pltpu.VMEM((128, width), F32), pltpu.VMEM((128, 256), F32)],
        )(qloc, qn, keys)
        ps.append(p)
        totals.append(total)

    vals, hyena, ss = kernel(
        vals_kernel,
        "vals",
        out_shape=(shape((32, 128, 256), BF), shape((32, 32, 128), BF), shape((32, 256), F32)),
        in_specs=[SMEM] + [ANY] * 8,
        out_specs=(VMEM, VMEM, VMEM),
        scratch_shapes=[pltpu.VMEM((1024, 128), F32), pltpu.SemaphoreType.DMA((8,))],
    )(info, *value_shards)
    ss = all_sum(ss)
    back = kernel(
        value_kernel,
        "value",
        out_shape=shape((32, 64, 128), BF),
        in_specs=[VMEM] * 12,
        out_specs=VMEM,
        scratch_shapes=[
            pltpu.VMEM((128, 8192), BF),
            pltpu.VMEM((1024, 128), F32),
            pltpu.VMEM((1024, 128), F32),
        ],
    )(ss, gain, vals, hyena, *ps, *totals)
    back = lax.all_to_all(back, "seq", 0, 0, tiled=True)
    return kernel(
        unpack_kernel,
        "unpack",
        out_shape=(shape((512, 256), BF), shape((256, 512), BF)),
        in_specs=[VMEM],
        out_specs=(VMEM, VMEM),
        scratch_shapes=[pltpu.VMEM((256, 128), F32)] * 2,
    )(back)


def solution(mesh):
    placed = (
        P("chan", "seq"),
        P("chan", "seq"),
        P("chan", "seq"),
        P(("chan", "seq"), None),
        P(("chan", "seq")),
        P(),
        P("seq", "chan"),
        P("seq", "chan"),
        P("chan"),
    )
    return jax.shard_map(
        local,
        mesh=mesh,
        in_specs=placed,
        out_specs=(P("chan", "seq"), P("seq", "chan")),
        check_vma=False,
    )
```

profile of v0, /device:TPU:2, one launch (start us, length us, event | category | flops | bytes accessed | tf_op | source)
XLA Modules:
  0.0 134.4 jit_solution(3899498243799863201)
XLA Ops:
  0.7 2.6 %shard_map.149 = bf16[32,128,128]{2,1,0:T(8,128)(2,1)} custom-call(bf16[512,256]{1,0:T(8,128)(2,1)} %hk.1, bf16[512,256]{1,0:T(8,128)(2,1)} %hv.1, bf16[512,256]{1,0:T(8,128)(2,1)} %hq.1, bf16[256,512]{1,0:T(8,128)(2,1)} %q.1, bf16[256,512]{1,0:T(8,128)(2,1)} %k.1), custom_call_target="tpu_custom_call" | custom-call | tf_op jit(solution)/shard_map/pallas_call | solution.py:379
  3.3 11.5 %all-to-all-start = ((bf16[32,128,128]{2,1,0:T(8,128)(2,1)}), bf16[32,128,128]{2,1,0:T(8,128)(2,1)S(1)}, u32[]{:S(2)}, u32[]{:S(2)}) async-start(bf16[32,128,128]{2,1,0:T(8,128)(2,1)} %shard_map.149), calls=%async_computation | async-start | bytes 2097152 | tf_op jit(solution)/shard_map/all_to_all | solution.py:389
  14.9 0.1 slice_reduce_fusion
  15.1 0.1 tile.10
  15.2 0.2 copy.20
  15.4 0.1 select_reduce_fusion
  15.4 0.1 concatenate.3.info
  15.6 2.6 %shard_map.150 = (f32[512,256]{1,0:T(8,128)S(1)}, f32[512,256]{1,0:T(8,128)S(1)}, bf16[128,32]{1,0:T(8,128)(2,1)S(1)}, bf16[64,64]{1,0:T(8,128)(2,1)S(1)}, f32[32,256]{1,0:T(8,128)S(1)}, /*index=5*/f32[32,256]{1,0:T(8,128)S(1)}) custom-call(f32[16,32,256]{2,1,0:T(8,128)S(1)} %bitcast.12, bf16[128,32]{1,0:T(8,128)(2,1)} %constant.104.clone.f1h, ...), custom_call_target="tpu_custom_call" | custom-call | tf_op jit(solution)/shard_map/pallas_call | solution.py:395
  18.2 24.6 %all-to-all-done.x = bf16[32,128,128]{2,1,0:T(8,128)(2,1)S(1)} async-done(((bf16[32,128,128]{2,1,0:T(8,128)(2,1)}), bf16[32,128,128]{2,1,0:T(8,128)(2,1)S(1)}, u32[]{:S(2)}, u32[]{:S(2)}) %all-to-all-start) | async-done | bytes 1048608 | tf_op jit(solution)/shard_map/all_to_all | solution.py:389
  42.8 5.0 %shard_map.151.rest_0_ = bf16[32,16,256]{2,1,0:T(8,128)(2,1)S(1)} custom-call(s32[72]{0:T(128)S(1)} %concatenate.3.info, bf16[32,128,128]{2,1,0:T(8,128)(2,1)S(1)} %all-to-all-done.x, f32[16]{0:T(128)S(1)} %copy-done.1, f32[512,256]{1,0:T(8,128)S(1)} %get-tuple-element.31.hr, f32[512,256]{1,0:T(8,128)S(1)} %get-tuple-element.32.hi, ...), custom_call_target="tpu_custom_call" | custom-call | tf_op jit(solution)/shard_map/pallas_call | solution.py:418
  47.8 1.0 collective-permute-start.3
  48.8 1.5 %collective-permute-start = (bf16[32,16,256]{2,1,0:T(8,128)(2,1)S(1)}, bf16[32,16,256]{2,1,0:T(8,128)(2,1)S(1)}, u32[]{:S(2)}, u32[]{:S(2)}) collective-permute-start(bf16[32,16,256]{2,1,0:T(8,128)(2,1)S(1)} %shard_map.151.rest_0_), channel_id=1, source_target_pairs={{0,8},{8,16},{16,24},{24,0},{32,40},{40,48},{48,56},{56,32},{64,72... | collective-permute-start | bytes 786440 | tf_op jit(solution)/shard_map/ppermute | solution.py:311
  50.3 4.0 %collective-permute-done.3.rest_4_ = bf16[32,16,256]{2,1,0:T(8,128)(2,1)S(1)} collective-permute-done((bf16[32,16,256]{2,1,0:T(8,128)(2,1)S(1)}, bf16[32,16,256]{2,1,0:T(8,128)(2,1)S(1)}, u32[]{:S(2)}, u32[]{:S(2)}) %collective-permute-start.3) | collective-permute-done | bytes 262176 | tf_op jit(solution)/shard_map/ppermute | solution.py:313
  54.3 3.2 %collective-permute-start.5 = (bf16[32,16,256]{2,1,0:T(8,128)(2,1)S(1)}, bf16[32,16,256]{2,1,0:T(8,128)(2,1)S(1)}, u32[]{:S(2)}, u32[]{:S(2)}) collective-permute-start(bf16[32,16,256]{2,1,0:T(8,128)(2,1)S(1)} %collective-permute-done.3.rest_4_), channel_id=1, source_target_pairs={{0,24},{8,0},{16,8},{24,16},{32,56},{40,32},{48,40},{56,48},{64,88... | collective-permute-start | bytes 786440 | tf_op jit(solution)/shard_map/ppermute | solution.py:316
  57.4 1.6 %shard_map.153 = (bf16[1024,128]{1,0:T(8,128)(2,1)S(1)}, bf16[1024,128]{1,0:T(8,128)(2,1)S(1)}) custom-call(s32[72]{0:T(128)S(1)} %concatenate.3.info, bf16[32,128,128]{2,1,0:T(8,128)(2,1)S(1)} %all-to-all-done.x), custom_call_target="tpu_custom_call" | custom-call | tf_op jit(solution)/shard_map/pallas_call | solution.py:408
  59.0 0.1 collective-permute-start.14
  59.1 3.2 %collective-permute-start.1 = (bf16[32,16,256]{2,1,0:T(8,128)(2,1)S(1)}, bf16[32,16,256]{2,1,0:T(8,128)(2,1)S(1)}, u32[]{:S(2)}, u32[]{:S(2)}) collective-permute-start(bf16[32,16,256]{2,1,0:T(8,128)(2,1)S(1)} %shard_map.151.rest_0_), channel_id=1, source_target_pairs={{0,24},{8,0},{16,8},{24,16},{32,56},{40,32},{48,40},{56,48},{64,88... | collective-permute-start | bytes 786440 | tf_op jit(solution)/shard_map/ppermute | solution.py:312
  62.3 1.2 collective-permute-start.4
  63.5 3.5 %collective-permute-start.6 = (bf16[32,16,256]{2,1,0:T(8,128)(2,1)S(1)}, bf16[32,16,256]{2,1,0:T(8,128)(2,1)S(1)}, u32[]{:S(2)}, u32[]{:S(2)}) collective-permute-start(bf16[32,16,256]{2,1,0:T(8,128)(2,1)S(1)} %collective-permute-done.5.rest_6_), channel_id=1, source_target_pairs={{0,24},{8,0},{16,8},{24,16},{32,56},{40,32},{48,40},{56,48},{64,88... | collective-permute-start | bytes 786440 | tf_op jit(solution)/shard_map/ppermute | solution.py:320
  67.0 1.5 %collective-permute-done.14.rest_1_ = bf16[1024,128]{1,0:T(8,128)(2,1)S(1)} collective-permute-done((bf16[1024,128]{1,0:T(8,128)(2,1)S(1)}, bf16[1024,128]{1,0:T(8,128)(2,1)S(1)}, u32[]{:S(2)}, u32[]{:S(2)}) %collective-permute-start.14) | collective-permute-done | bytes 262176 | tf_op jit(solution)/shard_map/ppermute | solution.py:311
  68.5 1.8 %collective-permute-start.17 = (bf16[1024,128]{1,0:T(8,128)(2,1)S(1)}, bf16[1024,128]{1,0:T(8,128)(2,1)S(1)}, u32[]{:S(2)}, u32[]{:S(2)}) collective-permute-start(bf16[1024,128]{1,0:T(8,128)(2,1)S(1)} %get-tuple-element.43.rest_0_), channel_id=1, source_target_pairs={{0,32},{8,40},{16,48},{24,56},{32,0},{40,8},{48,16},{56,24},{64,96... | collective-permute-start | bytes 786440 | tf_op jit(solution)/shard_map/ppermute | solution.py:313
  70.3 0.3 collective-permute-start.18
  70.5 0.8 collective-permute-done.2.rest_3_
  71.3 0.2 collective-permute-done.4.rest_5_
  71.5 1.0 collective-permute-done.6.rest_7_
  72.6 1.5 %shard_map.152 = (bf16[32,128,256]{2,1,0:T(8,128)(2,1)S(1)}, bf16[32,32,128]{2,1,0:T(8,128)(2,1)S(1)}, f32[32,256]{1,0:T(8,128)S(1)}) custom-call(s32[72]{0:T(128)S(1)} %concatenate.3.info, bf16[32,16,256]{2,1,0:T(8,128)(2,1)S(1)} %shard_map.151.rest_0_, bf16[32,16,256]{2,1,0:T(8,128)(2,1)S(1)} %collective-permute-done.rest_1_, ...), custom_call_target="tpu_custom_call" | custom-call | tf_op jit(solution)/shard_map/pallas_call | solution.py:453
  74.1 0.1 collective-permute-start.7
  74.2 1.2 collective-permute-done.7
  75.4 1.5 %collective-permute-start.10 = (f32[32,256]{1,0:T(8,128)S(1)}, f32[32,256]{1,0:T(8,128)S(1)}, u32[]{:S(2)}, u32[]{:S(2)}) collective-permute-start(f32[32,256]{1,0:T(8,128)S(1)} %add.132), channel_id=1, source_target_pairs={{0,6},{1,7},{2,4},{3,5},{4,2},{5,3},{6,0},{7,1},{8,14},{9,15},{10,... | collective-permute-start | bytes 98312 | tf_op jit(solution)/shard_map/ppermute | solution.py:327
  76.9 1.8 %collective-permute-start.8 = (f32[32,256]{1,0:T(8,128)S(1)}, f32[32,256]{1,0:T(8,128)S(1)}, u32[]{:S(2)}, u32[]{:S(2)}) collective-permute-start(f32[32,256]{1,0:T(8,128)S(1)} %add.132), channel_id=1, source_target_pairs={{0,2},{1,3},{2,0},{3,1},{4,6},{5,7},{6,4},{7,5},{8,10},{9,11},{10,... | collective-permute-start | bytes 98312 | tf_op jit(solution)/shard_map/ppermute | solution.py:327
  78.7 3.7 %collective-permute-start.15 = (bf16[1024,128]{1,0:T(8,128)(2,1)S(1)}, bf16[1024,128]{1,0:T(8,128)(2,1)S(1)}, u32[]{:S(2)}, u32[]{:S(2)}) collective-permute-start(bf16[1024,128]{1,0:T(8,128)(2,1)S(1)} %get-tuple-element.43.rest_0_), channel_id=1, source_target_pairs={{0,24},{8,0},{16,8},{24,16},{32,56},{40,32},{48,40},{56,48},{64,88... | collective-permute-start | bytes 786440 | tf_op jit(solution)/shard_map/ppermute | solution.py:312
  82.4 0.3 collective-permute-start.9
  82.7 3.1 %collective-permute-start.19 = (bf16[1024,128]{1,0:T(8,128)(2,1)S(1)}, bf16[1024,128]{1,0:T(8,128)(2,1)S(1)}, u32[]{:S(2)}, u32[]{:S(2)}) collective-permute-start(bf16[1024,128]{1,0:T(8,128)(2,1)S(1)} %collective-permute-done.17.rest_4_), channel_id=1, source_target_pairs={{0,24},{8,0},{16,8},{24,16},{32,56},{40,32},{48,40},{56,48},{64,88... | collective-permute-start | bytes 786440 | tf_op jit(solution)/shard_map/ppermute | solution.py:316
  85.8 2.1 %collective-permute-done.9 = f32[32,256]{1,0:T(8,128)S(1)} collective-permute-done((f32[32,256]{1,0:T(8,128)S(1)}, f32[32,256]{1,0:T(8,128)S(1)}, u32[]{:S(2)}, u32[]{:S(2)}) %collective-permute-start.9) | collective-permute-done | bytes 32800 | tf_op jit(solution)/shard_map/ppermute | solution.py:327
  87.9 0.3 collective-permute-start.11
  88.2 0.9 collective-permute-done.15.rest_2_
  89.1 3.5 %collective-permute-start.12 = (f32[32,256]{1,0:T(8,128)S(1)}, f32[32,256]{1,0:T(8,128)S(1)}, u32[]{:S(2)}, u32[]{:S(2)}) collective-permute-start(f32[32,256]{1,0:T(8,128)S(1)} %add_add_fusion.1), channel_id=1, source_target_pairs={{0,128},{8,136},{16,144},{24,152},{32,160},{40,168},{48,176},{56,1... | collective-permute-start | bytes 98312 | tf_op jit(solution)/shard_map/ppermute | solution.py:327
  92.6 0.2 collective-permute-done.16.rest_3_
  92.8 2.2 %collective-permute-start.13 = (f32[32,256]{1,0:T(8,128)S(1)}, f32[32,256]{1,0:T(8,128)S(1)}, u32[]{:S(2)}, u32[]{:S(2)}) collective-permute-start(f32[32,256]{1,0:T(8,128)S(1)} %add_add_fusion.1), channel_id=1, source_target_pairs={{0,192},{8,200},{16,208},{24,216},{32,224},{40,232},{48,240},{56,2... | collective-permute-start | bytes 98312 | tf_op jit(solution)/shard_map/ppermute | solution.py:327
  95.0 1.8 %collective-permute-done.20.rest_7_ = bf16[1024,128]{1,0:T(8,128)(2,1)S(1)} collective-permute-done((bf16[1024,128]{1,0:T(8,128)(2,1)S(1)}, bf16[1024,128]{1,0:T(8,128)(2,1)S(1)}, u32[]{:S(2)}, u32[]{:S(2)}) %collective-permute-start.20) | collective-permute-done | bytes 262176 | tf_op jit(solution)/shard_map/ppermute | solution.py:318
  96.8 0.8 shard_map.154.keys
  97.6 3.3 %shard_map.158 = (bf16[512,4096]{1,0:T(8,128)(2,1)S(1)}, f32[512,1]{1,0:T(8,128)S(1)}) custom-call(s32[128,1]{1,0:T(8,128)S(1)} %fusion.2.qloc, bf16[1024,128]{1,0:T(8,128)(2,1)S(1)} %get-tuple-element.42.q, bf16[8,1024,128]{2,1,0:T(8,128)(2,1)S(1)} %shard_map.154.keys), custom_call_target="tpu_custom_call" | custom-call | tf_op jit(solution)/shard_map/pallas_call | solution.py:442
  100.8 4.0 %shard_map.157 = (bf16[256,6144]{1,0:T(8,128)(2,1)S(1)}, f32[256,1]{1,0:T(8,128)S(1)}) custom-call(s32[128,1]{1,0:T(8,128)S(1)} %fusion.2.qloc, bf16[1024,128]{1,0:T(8,128)(2,1)S(1)} %get-tuple-element.42.q, bf16[8,1024,128]{2,1,0:T(8,128)(2,1)S(1)} %shard_map.154.keys), custom_call_target="tpu_custom_call" | custom-call | tf_op jit(solution)/shard_map/pallas_call | solution.py:442
  104.8 2.5 %shard_map.156 = (bf16[128,7168]{1,0:T(8,128)(2,1)S(1)}, f32[128,1]{1,0:T(8,128)S(1)}) custom-call(s32[128,1]{1,0:T(8,128)S(1)} %fusion.2.qloc, bf16[1024,128]{1,0:T(8,128)(2,1)S(1)} %get-tuple-element.42.q, bf16[8,1024,128]{2,1,0:T(8,128)(2,1)S(1)} %shard_map.154.keys), custom_call_target="tpu_custom_call" | custom-call | tf_op jit(solution)/shard_map/pallas_call | solution.py:442
  107.3 2.9 %shard_map.155 = (bf16[128,8192]{1,0:T(8,128)(2,1)S(1)}, f32[128,1]{1,0:T(8,128)S(1)}) custom-call(s32[128,1]{1,0:T(8,128)S(1)} %fusion.2.qloc, bf16[1024,128]{1,0:T(8,128)(2,1)S(1)} %get-tuple-element.42.q, bf16[8,1024,128]{2,1,0:T(8,128)(2,1)S(1)} %shard_map.154.keys), custom_call_target="tpu_custom_call" | custom-call | tf_op jit(solution)/shard_map/pallas_call | solution.py:442
  110.3 2.9 %shard_map.159 = bf16[32,64,128]{2,1,0:T(8,128)(2,1)S(1)} custom-call(f32[32,256]{1,0:T(8,128)S(1)} %add_add_fusion.ss, f32[1,128]{1,0:T(1,128)S(1)} %dynamic-slice_bitcast_fusion.gain, bf16[32,128,256]{2,1,0:T(8,128)(2,1)S(1)} %get-tuple-element.39.vals, bf16[32,32,128]{2,1,0:T(8,128)(2,1)S(1)} %get-tuple-element.40.hyena, ...), custom_call_target="tpu_custom_call" | custom-call | tf_op jit(solution)/shard_map/pallas_call | solution.py:462
  113.2 20.3 %all_to_all.10.x = bf16[32,64,128]{2,1,0:T(8,128)(2,1)S(1)} all-to-all(bf16[32,64,128]{2,1,0:T(8,128)(2,1)S(1)} %shard_map.159), channel_id=1, replica_groups=mesh['seq'=32,'chan'=8] {'seq'}, dimensions={0} | all-to-all | bytes 1048576 | tf_op jit(solution)/shard_map/all_to_all | solution.py:474
  133.5 1.0 shard_map.160
  (29 shorter events, 0.2 us)
Async XLA Ops:
  0.6 14.9 %copy-start = (f32[512]{0:T(512)S(1)}, f32[512]{0:T(512)}, u32[]{:S(2)}) copy-start(f32[512]{0:T(512)} %param.22) | copy-start | bytes 6148
  0.6 14.2 %copy-start.3 = (s32[8192]{0:T(1024)S(1)}, s32[8192]{0:T(1024)}, u32[]{:S(2)}) copy-start(s32[8192]{0:T(1024)} %param.19) | copy-start | bytes 98308
  0.7 14.5 %copy-start.2 = (f32[16,8192]{1,0:T(8,128)S(1)}, f32[16,8192]{1,0:T(8,128)}, u32[]{:S(2)}) copy-start(f32[16,8192]{1,0:T(8,128)} %param.17) | copy-start | bytes 1572868
  3.3 39.6 %copy-start.1 = (f32[16]{0:T(128)S(1)}, f32[16]{0:T(128)}, u32[]{:S(2)}) copy-start(f32[16]{0:T(128)} %skip.1) | copy-start | bytes 196
  3.3 39.6 %all-to-all-start = ((bf16[32,128,128]{2,1,0:T(8,128)(2,1)}), bf16[32,128,128]{2,1,0:T(8,128)(2,1)S(1)}, u32[]{:S(2)}, u32[]{:S(2)}) async-start(bf16[32,128,128]{2,1,0:T(8,128)(2,1)} %shard_map.149), calls=%async_computation | async-start | bytes 2097152 | tf_op jit(solution)/shard_map/all_to_all | solution.py:389
  47.8 6.5 %collective-permute-start.3 = (bf16[32,16,256]{2,1,0:T(8,128)(2,1)S(1)}, bf16[32,16,256]{2,1,0:T(8,128)(2,1)S(1)}, u32[]{:S(2)}, u32[]{:S(2)}) collective-permute-start(bf16[32,16,256]{2,1,0:T(8,128)(2,1)S(1)} %shard_map.151.rest_0_), channel_id=1, source_target_pairs={{0,32},{8,40},{16,48},{24,56},{32,0},{40,8},{48,16},{56,24},{64,96... | collective-permute-start | bytes 786440 | tf_op jit(solution)/shard_map/ppermute | solution.py:313
  48.8 13.5 %collective-permute-start = (bf16[32,16,256]{2,1,0:T(8,128)(2,1)S(1)}, bf16[32,16,256]{2,1,0:T(8,128)(2,1)S(1)}, u32[]{:S(2)}, u32[]{:S(2)}) collective-permute-start(bf16[32,16,256]{2,1,0:T(8,128)(2,1)S(1)} %shard_map.151.rest_0_), channel_id=1, source_target_pairs={{0,8},{8,16},{16,24},{24,0},{32,40},{40,48},{48,56},{56,32},{64,72... | collective-permute-start | bytes 786440 | tf_op jit(solution)/shard_map/ppermute | solution.py:311
  54.3 9.2 %collective-permute-start.5 = (bf16[32,16,256]{2,1,0:T(8,128)(2,1)S(1)}, bf16[32,16,256]{2,1,0:T(8,128)(2,1)S(1)}, u32[]{:S(2)}, u32[]{:S(2)}) collective-permute-start(bf16[32,16,256]{2,1,0:T(8,128)(2,1)S(1)} %collective-permute-done.3.rest_4_), channel_id=1, source_target_pairs={{0,24},{8,0},{16,8},{24,16},{32,56},{40,32},{48,40},{56,48},{64,88... | collective-permute-start | bytes 786440 | tf_op jit(solution)/shard_map/ppermute | solution.py:316
  59.0 9.5 %collective-permute-start.14 = (bf16[1024,128]{1,0:T(8,128)(2,1)S(1)}, bf16[1024,128]{1,0:T(8,128)(2,1)S(1)}, u32[]{:S(2)}, u32[]{:S(2)}) collective-permute-start(bf16[1024,128]{1,0:T(8,128)(2,1)S(1)} %get-tuple-element.43.rest_0_), channel_id=1, source_target_pairs={{0,8},{8,16},{16,24},{24,0},{32,40},{40,48},{48,56},{56,32},{64,72... | collective-permute-start | bytes 786440 | tf_op jit(solution)/shard_map/ppermute | solution.py:311
  59.1 11.2 %collective-permute-start.1 = (bf16[32,16,256]{2,1,0:T(8,128)(2,1)S(1)}, bf16[32,16,256]{2,1,0:T(8,128)(2,1)S(1)}, u32[]{:S(2)}, u32[]{:S(2)}) collective-permute-start(bf16[32,16,256]{2,1,0:T(8,128)(2,1)S(1)} %shard_map.151.rest_0_), channel_id=1, source_target_pairs={{0,24},{8,0},{16,8},{24,16},{32,56},{40,32},{48,40},{56,48},{64,88... | collective-permute-start | bytes 786440 | tf_op jit(solution)/shard_map/ppermute | solution.py:312
  62.3 9.0 %collective-permute-start.2 = (bf16[32,16,256]{2,1,0:T(8,128)(2,1)S(1)}, bf16[32,16,256]{2,1,0:T(8,128)(2,1)S(1)}, u32[]{:S(2)}, u32[]{:S(2)}) collective-permute-start(bf16[32,16,256]{2,1,0:T(8,128)(2,1)S(1)} %collective-permute-done.rest_1_), channel_id=1, source_target_pairs={{0,8},{8,16},{16,24},{24,0},{32,40},{40,48},{48,56},{56,32},{64,72... | collective-permute-start | bytes 786440 | tf_op jit(solution)/shard_map/ppermute | solution.py:314
  62.3 9.2 %collective-permute-start.4 = (bf16[32,16,256]{2,1,0:T(8,128)(2,1)S(1)}, bf16[32,16,256]{2,1,0:T(8,128)(2,1)S(1)}, u32[]{:S(2)}, u32[]{:S(2)}) collective-permute-start(bf16[32,16,256]{2,1,0:T(8,128)(2,1)S(1)} %collective-permute-done.rest_1_), channel_id=1, source_target_pairs={{0,32},{8,40},{16,48},{24,56},{32,0},{40,8},{48,16},{56,24},{64,96... | collective-permute-start | bytes 786440 | tf_op jit(solution)/shard_map/ppermute | solution.py:315
  63.5 9.1 %collective-permute-start.6 = (bf16[32,16,256]{2,1,0:T(8,128)(2,1)S(1)}, bf16[32,16,256]{2,1,0:T(8,128)(2,1)S(1)}, u32[]{:S(2)}, u32[]{:S(2)}) collective-permute-start(bf16[32,16,256]{2,1,0:T(8,128)(2,1)S(1)} %collective-permute-done.5.rest_6_), channel_id=1, source_target_pairs={{0,24},{8,0},{16,8},{24,16},{32,56},{40,32},{48,40},{56,48},{64,88... | collective-permute-start | bytes 786440 | tf_op jit(solution)/shard_map/ppermute | solution.py:320
  68.5 13.9 %collective-permute-start.17 = (bf16[1024,128]{1,0:T(8,128)(2,1)S(1)}, bf16[1024,128]{1,0:T(8,128)(2,1)S(1)}, u32[]{:S(2)}, u32[]{:S(2)}) collective-permute-start(bf16[1024,128]{1,0:T(8,128)(2,1)S(1)} %get-tuple-element.43.rest_0_), channel_id=1, source_target_pairs={{0,32},{8,40},{16,48},{24,56},{32,0},{40,8},{48,16},{56,24},{64,96... | collective-permute-start | bytes 786440 | tf_op jit(solution)/shard_map/ppermute | solution.py:313
  70.3 12.2 %collective-permute-start.18 = (bf16[1024,128]{1,0:T(8,128)(2,1)S(1)}, bf16[1024,128]{1,0:T(8,128)(2,1)S(1)}, u32[]{:S(2)}, u32[]{:S(2)}) collective-permute-start(bf16[1024,128]{1,0:T(8,128)(2,1)S(1)} %collective-permute-done.14.rest_1_), channel_id=1, source_target_pairs={{0,32},{8,40},{16,48},{24,56},{32,0},{40,8},{48,16},{56,24},{64,96... | collective-permute-start | bytes 786440 | tf_op jit(solution)/shard_map/ppermute | solution.py:315
  74.1 1.3 collective-permute-start.7
  75.4 7.3 %collective-permute-start.10 = (f32[32,256]{1,0:T(8,128)S(1)}, f32[32,256]{1,0:T(8,128)S(1)}, u32[]{:S(2)}, u32[]{:S(2)}) collective-permute-start(f32[32,256]{1,0:T(8,128)S(1)} %add.132), channel_id=1, source_target_pairs={{0,6},{1,7},{2,4},{3,5},{4,2},{5,3},{6,0},{7,1},{8,14},{9,15},{10,... | collective-permute-start | bytes 98312 | tf_op jit(solution)/shard_map/ppermute | solution.py:327
  76.9 8.9 %collective-permute-start.8 = (f32[32,256]{1,0:T(8,128)S(1)}, f32[32,256]{1,0:T(8,128)S(1)}, u32[]{:S(2)}, u32[]{:S(2)}) collective-permute-start(f32[32,256]{1,0:T(8,128)S(1)} %add.132), channel_id=1, source_target_pairs={{0,2},{1,3},{2,0},{3,1},{4,6},{5,7},{6,4},{7,5},{8,10},{9,11},{10,... | collective-permute-start | bytes 98312 | tf_op jit(solution)/shard_map/ppermute | solution.py:327
  78.7 10.4 %collective-permute-start.15 = (bf16[1024,128]{1,0:T(8,128)(2,1)S(1)}, bf16[1024,128]{1,0:T(8,128)(2,1)S(1)}, u32[]{:S(2)}, u32[]{:S(2)}) collective-permute-start(bf16[1024,128]{1,0:T(8,128)(2,1)S(1)} %get-tuple-element.43.rest_0_), channel_id=1, source_target_pairs={{0,24},{8,0},{16,8},{24,16},{32,56},{40,32},{48,40},{56,48},{64,88... | collective-permute-start | bytes 786440 | tf_op jit(solution)/shard_map/ppermute | solution.py:312
  82.4 10.4 %collective-permute-start.16 = (bf16[1024,128]{1,0:T(8,128)(2,1)S(1)}, bf16[1024,128]{1,0:T(8,128)(2,1)S(1)}, u32[]{:S(2)}, u32[]{:S(2)}) collective-permute-start(bf16[1024,128]{1,0:T(8,128)(2,1)S(1)} %collective-permute-done.14.rest_1_), channel_id=1, source_target_pairs={{0,8},{8,16},{16,24},{24,0},{32,40},{40,48},{48,56},{56,32},{64,72... | collective-permute-start | bytes 786440 | tf_op jit(solution)/shard_map/ppermute | solution.py:314
  82.4 5.5 %collective-permute-start.9 = (f32[32,256]{1,0:T(8,128)S(1)}, f32[32,256]{1,0:T(8,128)S(1)}, u32[]{:S(2)}, u32[]{:S(2)}) collective-permute-start(f32[32,256]{1,0:T(8,128)S(1)} %add.132), channel_id=1, source_target_pairs={{0,4},{1,5},{2,6},{3,7},{4,0},{5,1},{6,2},{7,3},{8,12},{9,13},{10,... | collective-permute-start | bytes 98312 | tf_op jit(solution)/shard_map/ppermute | solution.py:327
  82.7 12.3 %collective-permute-start.19 = (bf16[1024,128]{1,0:T(8,128)(2,1)S(1)}, bf16[1024,128]{1,0:T(8,128)(2,1)S(1)}, u32[]{:S(2)}, u32[]{:S(2)}) collective-permute-start(bf16[1024,128]{1,0:T(8,128)(2,1)S(1)} %collective-permute-done.17.rest_4_), channel_id=1, source_target_pairs={{0,24},{8,0},{16,8},{24,16},{32,56},{40,32},{48,40},{56,48},{64,88... | collective-permute-start | bytes 786440 | tf_op jit(solution)/shard_map/ppermute | solution.py:316
  85.8 10.9 %collective-permute-start.20 = (bf16[1024,128]{1,0:T(8,128)(2,1)S(1)}, bf16[1024,128]{1,0:T(8,128)(2,1)S(1)}, u32[]{:S(2)}, u32[]{:S(2)}) collective-permute-start(bf16[1024,128]{1,0:T(8,128)(2,1)S(1)} %collective-permute-done.18.rest_5_), channel_id=1, source_target_pairs={{0,8},{8,16},{16,24},{24,0},{32,40},{40,48},{48,56},{56,32},{64,72... | collective-permute-start | bytes 786440 | tf_op jit(solution)/shard_map/ppermute | solution.py:318
  87.9 22.3 %collective-permute-start.11 = (f32[32,256]{1,0:T(8,128)S(1)}, f32[32,256]{1,0:T(8,128)S(1)}, u32[]{:S(2)}, u32[]{:S(2)}) collective-permute-start(f32[32,256]{1,0:T(8,128)S(1)} %add_add_fusion.1), channel_id=1, source_target_pairs={{0,64},{8,72},{16,80},{24,88},{32,96},{40,104},{48,112},{56,120},{... | collective-permute-start | bytes 98312 | tf_op jit(solution)/shard_map/ppermute | solution.py:327
  89.1 21.1 %collective-permute-start.12 = (f32[32,256]{1,0:T(8,128)S(1)}, f32[32,256]{1,0:T(8,128)S(1)}, u32[]{:S(2)}, u32[]{:S(2)}) collective-permute-start(f32[32,256]{1,0:T(8,128)S(1)} %add_add_fusion.1), channel_id=1, source_target_pairs={{0,128},{8,136},{16,144},{24,152},{32,160},{40,168},{48,176},{56,1... | collective-permute-start | bytes 98312 | tf_op jit(solution)/shard_map/ppermute | solution.py:327
  92.8 17.4 %collective-permute-start.13 = (f32[32,256]{1,0:T(8,128)S(1)}, f32[32,256]{1,0:T(8,128)S(1)}, u32[]{:S(2)}, u32[]{:S(2)}) collective-permute-start(f32[32,256]{1,0:T(8,128)S(1)} %add_add_fusion.1), channel_id=1, source_target_pairs={{0,192},{8,200},{16,208},{24,216},{32,224},{40,232},{48,240},{56,2... | collective-permute-start | bytes 98312 | tf_op jit(solution)/shard_map/ppermute | solution.py:327
where the time goes:
time: 135 us; the launch traced here: 134 us
  starting transfers between devices  43.6 us (32%)
  waiting for transfers between devices  38.3 us (28%)
  Pallas kernels  30.6 us (23%)
  blocking collectives  20.3 us (15%)
    all_to_all x1, waiting for transfers between devices, local(): spread = lax.all_to_all(packed, 'seq', 0, 0, tiled=True)  24.6 us
    all_to_all x1, blocking collectives, local(): back = lax.all_to_all(back, 'seq', 0, 0, tiled=True)  20.3 us
    pallas_call x4, Pallas kernels, local(): kernel(functools.partial(score_kernel, tiles), 'score%d' % n, out_shape=(...  12.7 us
    all_to_all x1, starting transfers between devices, local(): spread = lax.all_to_all(packed, 'seq', 0, 0, tiled=True)  11.5 us
    ppermute x7, starting transfers between devices, all_sum(): lax.ppermute(x, axis, [(d, d ^ f) for d in range(size)])  9.6 us
    ppermute x2, starting transfers between devices, block_gather(): right = lax.ppermute(own, 'seq', down)  6.91 us
    ppermute x2, starting transfers between devices, block_gather(): other_right = lax.ppermute(other, 'seq', down)  6.31 us
    pallas_call x1, Pallas kernels, local(): kernel(conv_kernel, 'conv', out_shape=shape((32, 16, 256), BF), in_specs=...  4.96 us
  transfers between devices with their start and end apart: 22, of which 11 were waited for; matrix products, arithmetic and copies ran while one was open for 1% of the time, Pallas kernels for 14%

commit v1 on v0

--- a/solution.py
+++ b/solution.py
@@ -115,7 +115,7 @@
     hi[...] = (dot3(ii, w[0], w[1]) - dot3(rr, w[2], w[3])) * norm
 
 
-def conv_kernel(info, x, skip, hr, hi, f1, f2, tc, ts, wh, out, xs, qs, br, bi, w, sem):
+def conv_kernel(info, x, skip, hr, hi, f1, f2, tc, ts, wh, out, ss, xs, qs, br, bi, w, sem):
     table = pltpu.make_async_copy(wh, w, sem)
     table.start()
     for half in range(2):
@@ -141,6 +141,7 @@
     yi = split(xr * hi[...] + xi * hr[...])
     br[...] = dot3(yr, w[0], w[1]) - dot3(yi, w[2], w[3])
     bi[...] = dot3(yr, w[2], w[3]) + dot3(yi, w[0], w[1])
+    total = jnp.zeros((32, 256), F32)
     for c in range(16):
         gr = br[c * 32 : c * 32 + 32, :]
         gi = bi[c * 32 : c * 32 + 32, :]
@@ -150,8 +151,10 @@
         y = wide[:32] + wide[32:] + dot(f2[:32, :], dl)
         rows = pl.ds(c, 32, stride=16)
         g = (channel(qs, c) * (y + skip[c] * channel(xs, c))).astype(BF).astype(F32)
+        total = total + g * g
         qs[0, rows, :] = g[:, :128]
         qs[1, rows, :] = g[:, 128:]
+    ss[...] = total
     for half in range(2):
         lanes = slice(half * 128, half * 128 + 128)
         out[:, :, lanes] = qs[half].astype(BF).reshape(32, 16, 128)
@@ -238,7 +241,7 @@
 
 
 def vals_kernel(info, *rest):
-    shards, (vals, hyena, ss, hs, sem) = rest[:8], rest[8:]
+    shards, (vals, hyena, hs, sem) = rest[:8], rest[8:]
     copies = [
         pltpu.make_async_copy(
             shards[n], vals.at[:, pl.ds(pl.multiple_of(info[64 + n] * 16, 16), 16), :], sem.at[n]
@@ -249,9 +252,6 @@
         c.start()
     for c in copies:
         c.wait()
-    for a in range(32):
-        wide = vals[a].astype(F32)
-        ss[a : a + 1, :] = jnp.sum(wide * wide, axis=0, keepdims=True)
     own = info[64]
     for n in range(4):
         hs[n * 256 : n * 256 + 256, :] = vals[own * 4 + n].astype(F32).T
@@ -322,9 +322,17 @@
 
 
 def all_sum(x):
-    for axis, flips in (("chan", (1,)), ("chan", (2, 4, 6)), ("seq", (8, 16, 24))):
+    for axis, flips in (
+        ("chan", (1,)),
+        ("chan", (2, 4, 6)),
+        ("seq", (8, 16, 24)),
+        ("seq", (1, 2, 3)),
+        ("seq", (4,)),
+    ):
         size = 8 if axis == "chan" else 32
-        parts = [lax.ppermute(x, axis, [(d, d ^ f) for d in range(size)]) for f in flips]
+        parts = [
+            lax.ppermute(x, axis, [(d, d ^ f) for d in range(size)]) for f in flips
+        ]
         for part in parts:
             x = x + part
     return x
@@ -415,12 +423,12 @@
     )(info, spread)
     key_shards = block_gather("k", kn)
 
-    gated = kernel(
+    gated, ss = kernel(
         conv_kernel,
         "conv",
-        out_shape=shape((32, 16, 256), BF),
+        out_shape=(shape((32, 16, 256), BF), shape((32, 256), F32)),
         in_specs=[SMEM, VMEM, SMEM] + [VMEM] * 6 + [HBM],
-        out_specs=VMEM,
+        out_specs=(VMEM, VMEM),
         scratch_shapes=[pltpu.VMEM((2, 512, 128), F32)] * 2
         + [pltpu.VMEM((512, 256), F32)] * 2
         + [pltpu.VMEM((4, 256, 256), BF), pltpu.SemaphoreType.DMA],
@@ -450,12 +458,12 @@
         ps.append(p)
         totals.append(total)
 
-    vals, hyena, ss = kernel(
+    vals, hyena = kernel(
         vals_kernel,
         "vals",
-        out_shape=(shape((32, 128, 256), BF), shape((32, 32, 128), BF), shape((32, 256), F32)),
+        out_shape=(shape((32, 128, 256), BF), shape((32, 32, 128), BF)),
         in_specs=[SMEM] + [ANY] * 8,
-        out_specs=(VMEM, VMEM, VMEM),
+        out_specs=(VMEM, VMEM),
         scratch_shapes=[pltpu.VMEM((1024, 128), F32), pltpu.SemaphoreType.DMA((8,))],
     )(info, *value_shards)
     ss = all_sum(ss)

time: 135 us -> 146 us (1.081)
  the two profiles are of different devices: /device:TPU:2 before, /device:TPU:32 now
where the time goes in v1:
time: 146 us
  waiting for transfers between devices  47.1 us (32%)
  starting transfers between devices  46.8 us (32%)
  Pallas kernels  30.6 us (21%)
  blocking collectives  19.9 us (14%)
    all_to_all x1, waiting for transfers between devices, local(): spread = lax.all_to_all(packed, 'seq', 0, 0, tiled=True)  23.7 us
    all_to_all x1, blocking collectives, local(): back = lax.all_to_all(back, 'seq', 0, 0, tiled=True)  19.9 us
    ppermute x11, starting transfers between devices, all_sum(): lax.ppermute(x, axis, [(d, d ^ f) for d in range(size)])  18.3 us
    ppermute x11, waiting for transfers between devices, all_sum(): lax.ppermute(x, axis, [(d, d ^ f) for d in range(size)])  14.4 us
    pallas_call x4, Pallas kernels, local(): kernel(functools.partial(score_kernel, tiles), 'score%d' % n, out_shape=(...  12.7 us
    all_to_all x1, starting transfers between devices, local(): spread = lax.all_to_all(packed, 'seq', 0, 0, tiled=True)  11.4 us
    pallas_call x1, Pallas kernels, local(): kernel(conv_kernel, 'conv', out_shape=(shape((32, 16, 256), BF), shape((3...  5.12 us
    ppermute x2, waiting for transfers between devices, block_gather(): left = lax.ppermute(own, 'seq', up)  5.03 us
  transfers between devices with their start and end apart: 26, of which 8 were waited for; matrix products, arithmetic and copies ran while one was open for 0% of the time, Pallas kernels for 12%

profile of v1, /device:TPU:32, one launch (start us, length us, event | category | flops | bytes accessed | tf_op | source)
XLA Modules:
  0.0 146.1 jit_solution(8133774697670247855)
XLA Ops:
  0.7 2.6 %shard_map.149 = bf16[32,128,128]{2,1,0:T(8,128)(2,1)} custom-call(bf16[512,256]{1,0:T(8,128)(2,1)} %hk.1, bf16[512,256]{1,0:T(8,128)(2,1)} %hv.1, bf16[512,256]{1,0:T(8,128)(2,1)} %hq.1, bf16[256,512]{1,0:T(8,128)(2,1)} %q.1, bf16[256,512]{1,0:T(8,128)(2,1)} %k.1), custom_call_target="tpu_custom_call" | custom-call | tf_op jit(solution)/shard_map/pallas_call | solution.py:387
  3.2 11.4 %all-to-all-start = ((bf16[32,128,128]{2,1,0:T(8,128)(2,1)}), bf16[32,128,128]{2,1,0:T(8,128)(2,1)S(1)}, u32[]{:S(2)}, u32[]{:S(2)}) async-start(bf16[32,128,128]{2,1,0:T(8,128)(2,1)} %shard_map.149), calls=%async_computation | async-start | bytes 2097152 | tf_op jit(solution)/shard_map/all_to_all | solution.py:397
  14.8 0.1 slice_reduce_fusion
  14.9 0.1 tile.10
  15.0 0.2 copy.20
  15.2 0.1 select_reduce_fusion
  15.3 0.1 concatenate.3.info
  15.5 2.6 %shard_map.150 = (f32[512,256]{1,0:T(8,128)S(1)}, f32[512,256]{1,0:T(8,128)S(1)}, bf16[128,32]{1,0:T(8,128)(2,1)S(1)}, bf16[64,64]{1,0:T(8,128)(2,1)S(1)}, f32[32,256]{1,0:T(8,128)S(1)}, /*index=5*/f32[32,256]{1,0:T(8,128)S(1)}) custom-call(f32[16,32,256]{2,1,0:T(8,128)S(1)} %bitcast.12, bf16[128,32]{1,0:T(8,128)(2,1)} %constant.104.clone.f1h, ...), custom_call_target="tpu_custom_call" | custom-call | tf_op jit(solution)/shard_map/pallas_call | solution.py:403
  18.1 23.7 %all-to-all-done.x = bf16[32,128,128]{2,1,0:T(8,128)(2,1)S(1)} async-done(((bf16[32,128,128]{2,1,0:T(8,128)(2,1)}), bf16[32,128,128]{2,1,0:T(8,128)(2,1)S(1)}, u32[]{:S(2)}, u32[]{:S(2)}) %all-to-all-start) | async-done | bytes 1048608 | tf_op jit(solution)/shard_map/all_to_all | solution.py:397
  41.8 5.1 %shard_map.151 = (bf16[32,16,256]{2,1,0:T(8,128)(2,1)S(1)}, f32[32,256]{1,0:T(8,128)S(1)}) custom-call(s32[72]{0:T(128)S(1)} %concatenate.3.info, bf16[32,128,128]{2,1,0:T(8,128)(2,1)S(1)} %all-to-all-done.x, f32[16]{0:T(128)S(1)} %copy-done.1, f32[512,256]{1,0:T(8,128)S(1)} %get-tuple-element.32.hr, f32[512,256]{1,0:T(8,128)S(1)} %get-tuple-element.33.hi, ...), custom_call_target="tpu_custom_call" | custom-call | tf_op jit(solution)/shard_map/pallas_call | solution.py:426
  46.9 0.1 collective-permute-start
  47.0 1.2 collective-permute-done
  48.2 1.5 %collective-permute-start.1 = (f32[32,256]{1,0:T(8,128)S(1)}, f32[32,256]{1,0:T(8,128)S(1)}, u32[]{:S(2)}, u32[]{:S(2)}) collective-permute-start(f32[32,256]{1,0:T(8,128)S(1)} %add.144), channel_id=1, source_target_pairs={{0,2},{1,3},{2,0},{3,1},{4,6},{5,7},{6,4},{7,5},{8,10},{9,11},{10,... | collective-permute-start | bytes 98312 | tf_op jit(solution)/shard_map/ppermute | solution.py:334
  49.7 2.7 %collective-permute-start.2 = (f32[32,256]{1,0:T(8,128)S(1)}, f32[32,256]{1,0:T(8,128)S(1)}, u32[]{:S(2)}, u32[]{:S(2)}) collective-permute-start(f32[32,256]{1,0:T(8,128)S(1)} %add.144), channel_id=1, source_target_pairs={{0,4},{1,5},{2,6},{3,7},{4,0},{5,1},{6,2},{7,3},{8,12},{9,13},{10,... | collective-permute-start | bytes 98312 | tf_op jit(solution)/shard_map/ppermute | solution.py:334
  52.5 0.5 collective-permute-start.3
  52.9 2.2 %collective-permute-done.2 = f32[32,256]{1,0:T(8,128)S(1)} collective-permute-done((f32[32,256]{1,0:T(8,128)S(1)}, f32[32,256]{1,0:T(8,128)S(1)}, u32[]{:S(2)}, u32[]{:S(2)}) %collective-permute-start.2) | collective-permute-done | bytes 32800 | tf_op jit(solution)/shard_map/ppermute | solution.py:334
  55.1 2.4 %collective-permute-done.3 = f32[32,256]{1,0:T(8,128)S(1)} collective-permute-done((f32[32,256]{1,0:T(8,128)S(1)}, f32[32,256]{1,0:T(8,128)S(1)}, u32[]{:S(2)}, u32[]{:S(2)}) %collective-permute-start.3) | collective-permute-done | bytes 32800 | tf_op jit(solution)/shard_map/ppermute | solution.py:334
  57.6 2.0 %collective-permute-start.4 = (f32[32,256]{1,0:T(8,128)S(1)}, f32[32,256]{1,0:T(8,128)S(1)}, u32[]{:S(2)}, u32[]{:S(2)}) collective-permute-start(f32[32,256]{1,0:T(8,128)S(1)} %add_add_fusion.2), channel_id=1, source_target_pairs={{0,64},{8,72},{16,80},{24,88},{32,96},{40,104},{48,112},{56,120},{... | collective-permute-start | bytes 98312 | tf_op jit(solution)/shard_map/ppermute | solution.py:334
  59.6 1.5 %collective-permute-start.5 = (f32[32,256]{1,0:T(8,128)S(1)}, f32[32,256]{1,0:T(8,128)S(1)}, u32[]{:S(2)}, u32[]{:S(2)}) collective-permute-start(f32[32,256]{1,0:T(8,128)S(1)} %add_add_fusion.2), channel_id=1, source_target_pairs={{0,128},{8,136},{16,144},{24,152},{32,160},{40,168},{48,176},{56,1... | collective-permute-start | bytes 98312 | tf_op jit(solution)/shard_map/ppermute | solution.py:334
  61.2 3.0 %collective-permute-start.6 = (f32[32,256]{1,0:T(8,128)S(1)}, f32[32,256]{1,0:T(8,128)S(1)}, u32[]{:S(2)}, u32[]{:S(2)}) collective-permute-start(f32[32,256]{1,0:T(8,128)S(1)} %add_add_fusion.2), channel_id=1, source_target_pairs={{0,192},{8,200},{16,208},{24,216},{32,224},{40,232},{48,240},{56,2... | collective-permute-start | bytes 98312 | tf_op jit(solution)/shard_map/ppermute | solution.py:334
  64.2 3.3 %collective-permute-done.5 = f32[32,256]{1,0:T(8,128)S(1)} collective-permute-done((f32[32,256]{1,0:T(8,128)S(1)}, f32[32,256]{1,0:T(8,128)S(1)}, u32[]{:S(2)}, u32[]{:S(2)}) %collective-permute-start.5) | collective-permute-done | bytes 32800 | tf_op jit(solution)/shard_map/ppermute | solution.py:334
  67.5 0.2 collective-permute-start.7
  67.6 2.7 %collective-permute-start.8 = (f32[32,256]{1,0:T(8,128)S(1)}, f32[32,256]{1,0:T(8,128)S(1)}, u32[]{:S(2)}, u32[]{:S(2)}) collective-permute-start(f32[32,256]{1,0:T(8,128)S(1)} %add_add_fusion.1), channel_id=1, source_target_pairs={{0,16},{8,24},{16,0},{24,8},{32,48},{40,56},{48,32},{56,40},{64,80... | collective-permute-start | bytes 98312 | tf_op jit(solution)/shard_map/ppermute | solution.py:334
  70.3 1.9 %collective-permute-start.9 = (f32[32,256]{1,0:T(8,128)S(1)}, f32[32,256]{1,0:T(8,128)S(1)}, u32[]{:S(2)}, u32[]{:S(2)}) collective-permute-start(f32[32,256]{1,0:T(8,128)S(1)} %add_add_fusion.1), channel_id=1, source_target_pairs={{0,24},{8,16},{16,8},{24,0},{32,56},{40,48},{48,40},{56,32},{64,88... | collective-permute-start | bytes 98312 | tf_op jit(solution)/shard_map/ppermute | solution.py:334
  72.2 1.6 %shard_map.153 = (bf16[1024,128]{1,0:T(8,128)(2,1)S(1)}, bf16[1024,128]{1,0:T(8,128)(2,1)S(1)}) custom-call(s32[72]{0:T(128)S(1)} %concatenate.3.info, bf16[32,128,128]{2,1,0:T(8,128)(2,1)S(1)} %all-to-all-done.x), custom_call_target="tpu_custom_call" | custom-call | tf_op jit(solution)/shard_map/pallas_call | solution.py:416
  73.8 0.3 collective-permute-start.18
  74.1 2.4 %collective-permute-start.21 = (bf16[1024,128]{1,0:T(8,128)(2,1)S(1)}, bf16[1024,128]{1,0:T(8,128)(2,1)S(1)}, u32[]{:S(2)}, u32[]{:S(2)}) collective-permute-start(bf16[1024,128]{1,0:T(8,128)(2,1)S(1)} %get-tuple-element.45.rest_0_), channel_id=1, source_target_pairs={{0,32},{8,40},{16,48},{24,56},{32,0},{40,8},{48,16},{56,24},{64,96... | collective-permute-start | bytes 786440 | tf_op jit(solution)/shard_map/ppermute | solution.py:313
  76.5 3.1 %collective-permute-start.19 = (bf16[1024,128]{1,0:T(8,128)(2,1)S(1)}, bf16[1024,128]{1,0:T(8,128)(2,1)S(1)}, u32[]{:S(2)}, u32[]{:S(2)}) collective-permute-start(bf16[1024,128]{1,0:T(8,128)(2,1)S(1)} %get-tuple-element.45.rest_0_), channel_id=1, source_target_pairs={{0,24},{8,0},{16,8},{24,16},{32,56},{40,32},{48,40},{56,48},{64,88... | collective-permute-start | bytes 786440 | tf_op jit(solution)/shard_map/ppermute | solution.py:312
  79.7 2.1 %collective-permute-start.10 = (f32[32,256]{1,0:T(8,128)S(1)}, f32[32,256]{1,0:T(8,128)S(1)}, u32[]{:S(2)}, u32[]{:S(2)}) collective-permute-start(f32[32,256]{1,0:T(8,128)S(1)} %add_add_fusion), channel_id=1, source_target_pairs={{0,32},{8,40},{16,48},{24,56},{32,0},{40,8},{48,16},{56,24},{64,96... | collective-permute-start | bytes 98312 | tf_op jit(solution)/shard_map/ppermute | solution.py:334
  81.8 2.2 %collective-permute-start.22 = (bf16[1024,128]{1,0:T(8,128)(2,1)S(1)}, bf16[1024,128]{1,0:T(8,128)(2,1)S(1)}, u32[]{:S(2)}, u32[]{:S(2)}) collective-permute-start(bf16[1024,128]{1,0:T(8,128)(2,1)S(1)} %collective-permute-done.18.rest_1_), channel_id=1, source_target_pairs={{0,32},{8,40},{16,48},{24,56},{32,0},{40,8},{48,16},{56,24},{64,96... | collective-permute-start | bytes 786440 | tf_op jit(solution)/shard_map/ppermute | solution.py:315
  84.0 5.3 %collective-permute-done.10 = f32[32,256]{1,0:T(8,128)S(1)} collective-permute-done((f32[32,256]{1,0:T(8,128)S(1)}, f32[32,256]{1,0:T(8,128)S(1)}, u32[]{:S(2)}, u32[]{:S(2)}) %collective-permute-start.10) | collective-permute-done | bytes 32800 | tf_op jit(solution)/shard_map/ppermute | solution.py:334
  89.3 1.1 collective-permute-start.20
  90.4 2.2 %collective-permute-start.23 = (bf16[1024,128]{1,0:T(8,128)(2,1)S(1)}, bf16[1024,128]{1,0:T(8,128)(2,1)S(1)}, u32[]{:S(2)}, u32[]{:S(2)}) collective-permute-start(bf16[1024,128]{1,0:T(8,128)(2,1)S(1)} %collective-permute-done.21.rest_4_), channel_id=1, source_target_pairs={{0,24},{8,0},{16,8},{24,16},{32,56},{40,32},{48,40},{56,48},{64,88... | collective-permute-start | bytes 786440 | tf_op jit(solution)/shard_map/ppermute | solution.py:316
  92.6 1.9 %collective-permute-start.16 = (bf16[32,16,256]{2,1,0:T(8,128)(2,1)S(1)}, bf16[32,16,256]{2,1,0:T(8,128)(2,1)S(1)}, u32[]{:S(2)}, u32[]{:S(2)}) collective-permute-start(bf16[32,16,256]{2,1,0:T(8,128)(2,1)S(1)} %collective-permute-done.14.rest_4_), channel_id=1, source_target_pairs={{0,24},{8,0},{16,8},{24,16},{32,56},{40,32},{48,40},{56,48},{64,88... | collective-permute-start | bytes 786440 | tf_op jit(solution)/shard_map/ppermute | solution.py:316
  94.6 0.1 collective-permute-start.24
  94.7 5.0 %collective-permute-done.11.rest_1_ = bf16[32,16,256]{2,1,0:T(8,128)(2,1)S(1)} collective-permute-done((bf16[32,16,256]{2,1,0:T(8,128)(2,1)S(1)}, bf16[32,16,256]{2,1,0:T(8,128)(2,1)S(1)}, u32[]{:S(2)}, u32[]{:S(2)}) %collective-permute-start.11) | collective-permute-done | bytes 262176 | tf_op jit(solution)/shard_map/ppermute | solution.py:311
  99.7 0.3 collective-permute-start.12
  100.0 3.8 %collective-permute-done.20.rest_3_ = bf16[1024,128]{1,0:T(8,128)(2,1)S(1)} collective-permute-done((bf16[1024,128]{1,0:T(8,128)(2,1)S(1)}, bf16[1024,128]{1,0:T(8,128)(2,1)S(1)}, u32[]{:S(2)}, u32[]{:S(2)}) %collective-permute-start.20) | collective-permute-done | bytes 262176 | tf_op jit(solution)/shard_map/ppermute | solution.py:314
  103.8 3.5 %collective-permute-start.17 = (bf16[32,16,256]{2,1,0:T(8,128)(2,1)S(1)}, bf16[32,16,256]{2,1,0:T(8,128)(2,1)S(1)}, u32[]{:S(2)}, u32[]{:S(2)}) collective-permute-start(bf16[32,16,256]{2,1,0:T(8,128)(2,1)S(1)} %collective-permute-done.16.rest_6_), channel_id=1, source_target_pairs={{0,24},{8,0},{16,8},{24,16},{32,56},{40,32},{48,40},{56,48},{64,88... | collective-permute-start | bytes 786440 | tf_op jit(solution)/shard_map/ppermute | solution.py:320
  107.4 0.8 shard_map.154.keys
  108.1 3.3 %shard_map.158 = (bf16[512,4096]{1,0:T(8,128)(2,1)S(1)}, f32[512,1]{1,0:T(8,128)S(1)}) custom-call(s32[128,1]{1,0:T(8,128)S(1)} %fusion.2.qloc, bf16[1024,128]{1,0:T(8,128)(2,1)S(1)} %get-tuple-element.44.q, bf16[8,1024,128]{2,1,0:T(8,128)(2,1)S(1)} %shard_map.154.keys), custom_call_target="tpu_custom_call" | custom-call | tf_op jit(solution)/shard_map/pallas_call | solution.py:450
  111.4 4.0 %shard_map.157 = (bf16[256,6144]{1,0:T(8,128)(2,1)S(1)}, f32[256,1]{1,0:T(8,128)S(1)}) custom-call(s32[128,1]{1,0:T(8,128)S(1)} %fusion.2.qloc, bf16[1024,128]{1,0:T(8,128)(2,1)S(1)} %get-tuple-element.44.q, bf16[8,1024,128]{2,1,0:T(8,128)(2,1)S(1)} %shard_map.154.keys), custom_call_target="tpu_custom_call" | custom-call | tf_op jit(solution)/shard_map/pallas_call | solution.py:450
  115.4 2.5 %shard_map.156 = (bf16[128,7168]{1,0:T(8,128)(2,1)S(1)}, f32[128,1]{1,0:T(8,128)S(1)}) custom-call(s32[128,1]{1,0:T(8,128)S(1)} %fusion.2.qloc, bf16[1024,128]{1,0:T(8,128)(2,1)S(1)} %get-tuple-element.44.q, bf16[8,1024,128]{2,1,0:T(8,128)(2,1)S(1)} %shard_map.154.keys), custom_call_target="tpu_custom_call" | custom-call | tf_op jit(solution)/shard_map/pallas_call | solution.py:450
  117.9 2.9 %shard_map.155 = (bf16[128,8192]{1,0:T(8,128)(2,1)S(1)}, f32[128,1]{1,0:T(8,128)S(1)}) custom-call(s32[128,1]{1,0:T(8,128)S(1)} %fusion.2.qloc, bf16[1024,128]{1,0:T(8,128)(2,1)S(1)} %get-tuple-element.44.q, bf16[8,1024,128]{2,1,0:T(8,128)(2,1)S(1)} %shard_map.154.keys), custom_call_target="tpu_custom_call" | custom-call | tf_op jit(solution)/shard_map/pallas_call | solution.py:450
  120.9 1.5 %shard_map.152 = (bf16[32,128,256]{2,1,0:T(8,128)(2,1)S(1)}, bf16[32,32,128]{2,1,0:T(8,128)(2,1)S(1)}) custom-call(s32[72]{0:T(128)S(1)} %concatenate.3.info, bf16[32,16,256]{2,1,0:T(8,128)(2,1)S(1)} %get-tuple-element.40.rest_0_, bf16[32,16,256]{2,1,0:T(8,128)(2,1)S(1)} %collective-permute-done.11.rest_1_, ...), custom_call_target="tpu_custom_call" | custom-call | tf_op jit(solution)/shard_map/pallas_call | solution.py:461
  122.3 2.9 %shard_map.159 = bf16[32,64,128]{2,1,0:T(8,128)(2,1)S(1)} custom-call(f32[32,256]{1,0:T(8,128)S(1)} %add.154.ss, f32[1,128]{1,0:T(1,128)S(1)} %dynamic-slice_bitcast_fusion.gain, bf16[32,128,256]{2,1,0:T(8,128)(2,1)S(1)} %get-tuple-element.41.vals, bf16[32,32,128]{2,1,0:T(8,128)(2,1)S(1)} %get-tuple-element.42.hyena, ...), custom_call_target="tpu_custom_call" | custom-call | tf_op jit(solution)/shard_map/pallas_call | solution.py:470
  125.2 19.9 %all_to_all.10.x = bf16[32,64,128]{2,1,0:T(8,128)(2,1)S(1)} all-to-all(bf16[32,64,128]{2,1,0:T(8,128)(2,1)S(1)} %shard_map.159), channel_id=1, replica_groups=mesh['seq'=32,'chan'=8] {'seq'}, dimensions={0} | all-to-all | bytes 1048576 | tf_op jit(solution)/shard_map/all_to_all | solution.py:482
  145.1 1.0 shard_map.160
  (39 shorter events, 0.2 us)
Async XLA Ops:
  0.6 14.7 %copy-start = (f32[512]{0:T(512)S(1)}, f32[512]{0:T(512)}, u32[]{:S(2)}) copy-start(f32[512]{0:T(512)} %param.22) | copy-start | bytes 6148
  0.6 14.1 %copy-start.3 = (s32[8192]{0:T(1024)S(1)}, s32[8192]{0:T(1024)}, u32[]{:S(2)}) copy-start(s32[8192]{0:T(1024)} %param.19) | copy-start | bytes 98308
  0.7 14.4 %copy-start.2 = (f32[16,8192]{1,0:T(8,128)S(1)}, f32[16,8192]{1,0:T(8,128)}, u32[]{:S(2)}) copy-start(f32[16,8192]{1,0:T(8,128)} %param.17) | copy-start | bytes 1572868
  3.2 38.6 %copy-start.1 = (f32[16]{0:T(128)S(1)}, f32[16]{0:T(128)}, u32[]{:S(2)}) copy-start(f32[16]{0:T(128)} %skip.1) | copy-start | bytes 196
  3.2 38.6 %all-to-all-start = ((bf16[32,128,128]{2,1,0:T(8,128)(2,1)}), bf16[32,128,128]{2,1,0:T(8,128)(2,1)S(1)}, u32[]{:S(2)}, u32[]{:S(2)}) async-start(bf16[32,128,128]{2,1,0:T(8,128)(2,1)} %shard_map.149), calls=%async_computation | async-start | bytes 2097152 | tf_op jit(solution)/shard_map/all_to_all | solution.py:397
  46.9 1.3 collective-permute-start
  48.2 4.7 %collective-permute-start.1 = (f32[32,256]{1,0:T(8,128)S(1)}, f32[32,256]{1,0:T(8,128)S(1)}, u32[]{:S(2)}, u32[]{:S(2)}) collective-permute-start(f32[32,256]{1,0:T(8,128)S(1)} %add.144), channel_id=1, source_target_pairs={{0,2},{1,3},{2,0},{3,1},{4,6},{5,7},{6,4},{7,5},{8,10},{9,11},{10,... | collective-permute-start | bytes 98312 | tf_op jit(solution)/shard_map/ppermute | solution.py:334
  49.7 5.4 %collective-permute-start.2 = (f32[32,256]{1,0:T(8,128)S(1)}, f32[32,256]{1,0:T(8,128)S(1)}, u32[]{:S(2)}, u32[]{:S(2)}) collective-permute-start(f32[32,256]{1,0:T(8,128)S(1)} %add.144), channel_id=1, source_target_pairs={{0,4},{1,5},{2,6},{3,7},{4,0},{5,1},{6,2},{7,3},{8,12},{9,13},{10,... | collective-permute-start | bytes 98312 | tf_op jit(solution)/shard_map/ppermute | solution.py:334
  52.5 5.1 %collective-permute-start.3 = (f32[32,256]{1,0:T(8,128)S(1)}, f32[32,256]{1,0:T(8,128)S(1)}, u32[]{:S(2)}, u32[]{:S(2)}) collective-permute-start(f32[32,256]{1,0:T(8,128)S(1)} %add.144), channel_id=1, source_target_pairs={{0,6},{1,7},{2,4},{3,5},{4,2},{5,3},{6,0},{7,1},{8,14},{9,15},{10,... | collective-permute-start | bytes 98312 | tf_op jit(solution)/shard_map/ppermute | solution.py:334
  57.6 6.6 %collective-permute-start.4 = (f32[32,256]{1,0:T(8,128)S(1)}, f32[32,256]{1,0:T(8,128)S(1)}, u32[]{:S(2)}, u32[]{:S(2)}) collective-permute-start(f32[32,256]{1,0:T(8,128)S(1)} %add_add_fusion.2), channel_id=1, source_target_pairs={{0,64},{8,72},{16,80},{24,88},{32,96},{40,104},{48,112},{56,120},{... | collective-permute-start | bytes 98312 | tf_op jit(solution)/shard_map/ppermute | solution.py:334
  59.6 7.8 %collective-permute-start.5 = (f32[32,256]{1,0:T(8,128)S(1)}, f32[32,256]{1,0:T(8,128)S(1)}, u32[]{:S(2)}, u32[]{:S(2)}) collective-permute-start(f32[32,256]{1,0:T(8,128)S(1)} %add_add_fusion.2), channel_id=1, source_target_pairs={{0,128},{8,136},{16,144},{24,152},{32,160},{40,168},{48,176},{56,1... | collective-permute-start | bytes 98312 | tf_op jit(solution)/shard_map/ppermute | solution.py:334
  61.2 6.3 %collective-permute-start.6 = (f32[32,256]{1,0:T(8,128)S(1)}, f32[32,256]{1,0:T(8,128)S(1)}, u32[]{:S(2)}, u32[]{:S(2)}) collective-permute-start(f32[32,256]{1,0:T(8,128)S(1)} %add_add_fusion.2), channel_id=1, source_target_pairs={{0,192},{8,200},{16,208},{24,216},{32,224},{40,232},{48,240},{56,2... | collective-permute-start | bytes 98312 | tf_op jit(solution)/shard_map/ppermute | solution.py:334
  67.5 9.0 %collective-permute-start.7 = (f32[32,256]{1,0:T(8,128)S(1)}, f32[32,256]{1,0:T(8,128)S(1)}, u32[]{:S(2)}, u32[]{:S(2)}) collective-permute-start(f32[32,256]{1,0:T(8,128)S(1)} %add_add_fusion.1), channel_id=1, source_target_pairs={{0,8},{8,0},{16,24},{24,16},{32,40},{40,32},{48,56},{56,48},{64,72... | collective-permute-start | bytes 98312 | tf_op jit(solution)/shard_map/ppermute | solution.py:334
  67.6 12.0 %collective-permute-start.8 = (f32[32,256]{1,0:T(8,128)S(1)}, f32[32,256]{1,0:T(8,128)S(1)}, u32[]{:S(2)}, u32[]{:S(2)}) collective-permute-start(f32[32,256]{1,0:T(8,128)S(1)} %add_add_fusion.1), channel_id=1, source_target_pairs={{0,16},{8,24},{16,0},{24,8},{32,48},{40,56},{48,32},{56,40},{64,80... | collective-permute-start | bytes 98312 | tf_op jit(solution)/shard_map/ppermute | solution.py:334
  70.3 9.3 %collective-permute-start.9 = (f32[32,256]{1,0:T(8,128)S(1)}, f32[32,256]{1,0:T(8,128)S(1)}, u32[]{:S(2)}, u32[]{:S(2)}) collective-permute-start(f32[32,256]{1,0:T(8,128)S(1)} %add_add_fusion.1), channel_id=1, source_target_pairs={{0,24},{8,16},{16,8},{24,0},{32,56},{40,48},{48,40},{56,32},{64,88... | collective-permute-start | bytes 98312 | tf_op jit(solution)/shard_map/ppermute | solution.py:334
  73.8 8.0 %collective-permute-start.18 = (bf16[1024,128]{1,0:T(8,128)(2,1)S(1)}, bf16[1024,128]{1,0:T(8,128)(2,1)S(1)}, u32[]{:S(2)}, u32[]{:S(2)}) collective-permute-start(bf16[1024,128]{1,0:T(8,128)(2,1)S(1)} %get-tuple-element.45.rest_0_), channel_id=1, source_target_pairs={{0,8},{8,16},{16,24},{24,0},{32,40},{40,48},{48,56},{56,32},{64,72... | collective-permute-start | bytes 786440 | tf_op jit(solution)/shard_map/ppermute | solution.py:311
  74.1 15.2 %collective-permute-start.21 = (bf16[1024,128]{1,0:T(8,128)(2,1)S(1)}, bf16[1024,128]{1,0:T(8,128)(2,1)S(1)}, u32[]{:S(2)}, u32[]{:S(2)}) collective-permute-start(bf16[1024,128]{1,0:T(8,128)(2,1)S(1)} %get-tuple-element.45.rest_0_), channel_id=1, source_target_pairs={{0,32},{8,40},{16,48},{24,56},{32,0},{40,8},{48,16},{56,24},{64,96... | collective-permute-start | bytes 786440 | tf_op jit(solution)/shard_map/ppermute | solution.py:313
  76.5 13.9 %collective-permute-start.19 = (bf16[1024,128]{1,0:T(8,128)(2,1)S(1)}, bf16[1024,128]{1,0:T(8,128)(2,1)S(1)}, u32[]{:S(2)}, u32[]{:S(2)}) collective-permute-start(bf16[1024,128]{1,0:T(8,128)(2,1)S(1)} %get-tuple-element.45.rest_0_), channel_id=1, source_target_pairs={{0,24},{8,0},{16,8},{24,16},{32,56},{40,32},{48,40},{56,48},{64,88... | collective-permute-start | bytes 786440 | tf_op jit(solution)/shard_map/ppermute | solution.py:312
  79.6 13.0 %collective-permute-start.14 = (bf16[32,16,256]{2,1,0:T(8,128)(2,1)S(1)}, bf16[32,16,256]{2,1,0:T(8,128)(2,1)S(1)}, u32[]{:S(2)}, u32[]{:S(2)}) collective-permute-start(bf16[32,16,256]{2,1,0:T(8,128)(2,1)S(1)} %get-tuple-element.40.rest_0_), channel_id=1, source_target_pairs={{0,32},{8,40},{16,48},{24,56},{32,0},{40,8},{48,16},{56,24},{64,96... | collective-permute-start | bytes 786440 | tf_op jit(solution)/shard_map/ppermute | solution.py:313
  79.7 9.6 %collective-permute-start.10 = (f32[32,256]{1,0:T(8,128)S(1)}, f32[32,256]{1,0:T(8,128)S(1)}, u32[]{:S(2)}, u32[]{:S(2)}) collective-permute-start(f32[32,256]{1,0:T(8,128)S(1)} %add_add_fusion), channel_id=1, source_target_pairs={{0,32},{8,40},{16,48},{24,56},{32,0},{40,8},{48,16},{56,24},{64,96... | collective-permute-start | bytes 98312 | tf_op jit(solution)/shard_map/ppermute | solution.py:334
  81.8 12.8 %collective-permute-start.22 = (bf16[1024,128]{1,0:T(8,128)(2,1)S(1)}, bf16[1024,128]{1,0:T(8,128)(2,1)S(1)}, u32[]{:S(2)}, u32[]{:S(2)}) collective-permute-start(bf16[1024,128]{1,0:T(8,128)(2,1)S(1)} %collective-permute-done.18.rest_1_), channel_id=1, source_target_pairs={{0,32},{8,40},{16,48},{24,56},{32,0},{40,8},{48,16},{56,24},{64,96... | collective-permute-start | bytes 786440 | tf_op jit(solution)/shard_map/ppermute | solution.py:315
  89.3 10.4 %collective-permute-start.11 = (bf16[32,16,256]{2,1,0:T(8,128)(2,1)S(1)}, bf16[32,16,256]{2,1,0:T(8,128)(2,1)S(1)}, u32[]{:S(2)}, u32[]{:S(2)}) collective-permute-start(bf16[32,16,256]{2,1,0:T(8,128)(2,1)S(1)} %get-tuple-element.40.rest_0_), channel_id=1, source_target_pairs={{0,8},{8,16},{16,24},{24,0},{32,40},{40,48},{48,56},{56,32},{64,72... | collective-permute-start | bytes 786440 | tf_op jit(solution)/shard_map/ppermute | solution.py:311
  89.3 14.5 %collective-permute-start.20 = (bf16[1024,128]{1,0:T(8,128)(2,1)S(1)}, bf16[1024,128]{1,0:T(8,128)(2,1)S(1)}, u32[]{:S(2)}, u32[]{:S(2)}) collective-permute-start(bf16[1024,128]{1,0:T(8,128)(2,1)S(1)} %collective-permute-done.18.rest_1_), channel_id=1, source_target_pairs={{0,8},{8,16},{16,24},{24,0},{32,40},{40,48},{48,56},{56,32},{64,72... | collective-permute-start | bytes 786440 | tf_op jit(solution)/shard_map/ppermute | solution.py:314
  90.4 13.4 %collective-permute-start.23 = (bf16[1024,128]{1,0:T(8,128)(2,1)S(1)}, bf16[1024,128]{1,0:T(8,128)(2,1)S(1)}, u32[]{:S(2)}, u32[]{:S(2)}) collective-permute-start(bf16[1024,128]{1,0:T(8,128)(2,1)S(1)} %collective-permute-done.21.rest_4_), channel_id=1, source_target_pairs={{0,24},{8,0},{16,8},{24,16},{32,56},{40,32},{48,40},{56,48},{64,88... | collective-permute-start | bytes 786440 | tf_op jit(solution)/shard_map/ppermute | solution.py:316
  92.6 11.2 %collective-permute-start.16 = (bf16[32,16,256]{2,1,0:T(8,128)(2,1)S(1)}, bf16[32,16,256]{2,1,0:T(8,128)(2,1)S(1)}, u32[]{:S(2)}, u32[]{:S(2)}) collective-permute-start(bf16[32,16,256]{2,1,0:T(8,128)(2,1)S(1)} %collective-permute-done.14.rest_4_), channel_id=1, source_target_pairs={{0,24},{8,0},{16,8},{24,16},{32,56},{40,32},{48,40},{56,48},{64,88... | collective-permute-start | bytes 786440 | tf_op jit(solution)/shard_map/ppermute | solution.py:316
  94.6 12.8 %collective-permute-start.24 = (bf16[1024,128]{1,0:T(8,128)(2,1)S(1)}, bf16[1024,128]{1,0:T(8,128)(2,1)S(1)}, u32[]{:S(2)}, u32[]{:S(2)}) collective-permute-start(bf16[1024,128]{1,0:T(8,128)(2,1)S(1)} %collective-permute-done.22.rest_5_), channel_id=1, source_target_pairs={{0,8},{8,16},{16,24},{24,0},{32,40},{40,48},{48,56},{56,32},{64,72... | collective-permute-start | bytes 786440 | tf_op jit(solution)/shard_map/ppermute | solution.py:318
  99.7 21.1 %collective-permute-start.12 = (bf16[32,16,256]{2,1,0:T(8,128)(2,1)S(1)}, bf16[32,16,256]{2,1,0:T(8,128)(2,1)S(1)}, u32[]{:S(2)}, u32[]{:S(2)}) collective-permute-start(bf16[32,16,256]{2,1,0:T(8,128)(2,1)S(1)} %get-tuple-element.40.rest_0_), channel_id=1, source_target_pairs={{0,24},{8,0},{16,8},{24,16},{32,56},{40,32},{48,40},{56,48},{64,88... | collective-permute-start | bytes 786440 | tf_op jit(solution)/shard_map/ppermute | solution.py:312
  103.8 17.0 %collective-permute-start.13 = (bf16[32,16,256]{2,1,0:T(8,128)(2,1)S(1)}, bf16[32,16,256]{2,1,0:T(8,128)(2,1)S(1)}, u32[]{:S(2)}, u32[]{:S(2)}) collective-permute-start(bf16[32,16,256]{2,1,0:T(8,128)(2,1)S(1)} %collective-permute-done.11.rest_1_), channel_id=1, source_target_pairs={{0,8},{8,16},{16,24},{24,0},{32,40},{40,48},{48,56},{56,32},{64,72... | collective-permute-start | bytes 786440 | tf_op jit(solution)/shard_map/ppermute | solution.py:314
  103.8 17.0 %collective-permute-start.15 = (bf16[32,16,256]{2,1,0:T(8,128)(2,1)S(1)}, bf16[32,16,256]{2,1,0:T(8,128)(2,1)S(1)}, u32[]{:S(2)}, u32[]{:S(2)}) collective-permute-start(bf16[32,16,256]{2,1,0:T(8,128)(2,1)S(1)} %collective-permute-done.11.rest_1_), channel_id=1, source_target_pairs={{0,32},{8,40},{16,48},{24,56},{32,0},{40,8},{48,16},{56,24},{64,96... | collective-permute-start | bytes 786440 | tf_op jit(solution)/shard_map/ppermute | solution.py:315
  103.8 17.0 %collective-permute-start.17 = (bf16[32,16,256]{2,1,0:T(8,128)(2,1)S(1)}, bf16[32,16,256]{2,1,0:T(8,128)(2,1)S(1)}, u32[]{:S(2)}, u32[]{:S(2)}) collective-permute-start(bf16[32,16,256]{2,1,0:T(8,128)(2,1)S(1)} %collective-permute-done.16.rest_6_), channel_id=1, source_target_pairs={{0,24},{8,0},{16,8},{24,16},{32,56},{40,32},{48,40},{56,48},{64,88... | collective-permute-start | bytes 786440 | tf_op jit(solution)/shard_map/ppermute | solution.py:320

commit v2 on v1

--- a/solution.py
+++ b/solution.py
@@ -115,9 +115,7 @@
     hi[...] = (dot3(ii, w[0], w[1]) - dot3(rr, w[2], w[3])) * norm
 
 
-def conv_kernel(info, x, skip, hr, hi, f1, f2, tc, ts, wh, out, ss, xs, qs, br, bi, w, sem):
-    table = pltpu.make_async_copy(wh, w, sem)
-    table.start()
+def conv_kernel(info, x, skip, hr, hi, f1, f2, tc, ts, w, out, ss, xs, qs, br, bi):
     for half in range(2):
         xs[half] = x[:, half * 16 : half * 16 + 16, :].reshape(512, 128).astype(F32)
         qs[half] = x[:, half * 16 + 32 : half * 16 + 48, :].reshape(512, 128).astype(F32)
@@ -132,7 +130,6 @@
         ar, ai = a[:32], a[32:]
         br[c * 32 : c * 32 + 32, :] = ar * tc[...] + ai * ts[...]
         bi[c * 32 : c * 32 + 32, :] = ai * tc[...] - ar * ts[...]
-    table.wait()
     rr = split(br[...])
     ii = split(bi[...])
     xr = dot3(rr, w[0], w[1]) + dot3(ii, w[2], w[3])
@@ -160,13 +157,16 @@
         out[:, :, lanes] = qs[half].astype(BF).reshape(32, 16, 128)
 
 
-def order_kernel(info, x, kout, qout, ks, qs):
+def order_kernel(info, x, wh, kout, qout, w, ks, qs, sem):
+    table = pltpu.make_async_copy(wh, w, sem)
+    table.start()
     for r in range(32):
         ks[pl.ds(r, 32, stride=32), :] = x[info[32 + r], 96:128, :].astype(F32)
     kout[...] = ks[...].astype(BF)
     for s in range(32):
         qs[pl.ds(s, 32, stride=32), :] = x[s, 64:96, :].astype(F32)
     qout[...] = qs[...].astype(BF)
+    table.wait()
 
 
 def keys_kernel(info, *rest):
@@ -196,17 +196,23 @@
             return lax.dot_general(query, kb, NT, preferred_element_type=F32)
 
         def columns(chunk, quarter):
-            return pl.ds(pl.multiple_of(chunk * 1024 + quarter * 256, 256), 256)
-
-        def plain(chunk, top):
-            for quarter in range(4):
-                v = scores(chunk, quarter)
+            start = chunk * 1024 + quarter * 256
+            if isinstance(start, int):
+                return slice(start, start + 256)
+            return pl.ds(pl.multiple_of(start, 256), 256)
+
+        def plain(chunk, top, count=1):
+            for quarter in range(4 * count):
+                v = scores(chunk + quarter // 4, quarter % 4)
                 s[:, columns(chunk, quarter)] = v
                 top = jnp.maximum(top, v)
             return top
 
         top = jnp.full((128, 256), -1e30, F32)
-        top = lax.fori_loop(0, tile, plain, top)
+        if tile > 1:
+            top = lax.fori_loop(0, tile // 2, lambda n, x: plain(2 * n, x, 2), top)
+        if tile % 2:
+            top = plain(tile - 1, top)
         peak[...] = top
         for quarter in range(4):
             low = quarter * 32
@@ -220,15 +226,20 @@
         top = peak[...]
         top = jnp.max(top, axis=1, keepdims=True)
 
-        def weigh(chunk, acc):
-            for quarter in range(4):
+        def weigh(chunk, acc, count=1):
+            for quarter in range(4 * count):
                 cols = columns(chunk, quarter)
                 e = jnp.exp2((s[:, cols] - top) * scale)
                 p[base : base + 128, cols] = e.astype(BF)
                 acc = acc + e
             return acc
 
-        peak[...] = lax.fori_loop(0, tile, weigh, jnp.zeros((128, 256), F32))
+        acc = jnp.zeros((128, 256), F32)
+        if tile > 1:
+            acc = lax.fori_loop(0, tile // 2, lambda n, x: weigh(2 * n, x, 2), acc)
+        if tile % 2:
+            acc = weigh(tile - 1, acc)
+        peak[...] = acc
         for quarter in range(4):
             low = quarter * 32
             start = tile * 1024 + quarter * 256
@@ -413,26 +424,25 @@
     )(long_filter, *(in_hbm(t[n]) for n in ("f1", "f2", "tc", "ts", "w")))
     spread, hr = lax.optimization_barrier((spread, hr))
 
-    kn, qn = kernel(
+    kn, qn, w = kernel(
         order_kernel,
         "order",
-        out_shape=(shape((1024, 128), BF), shape((1024, 128), BF)),
-        in_specs=[SMEM, VMEM],
-        out_specs=(VMEM, VMEM),
-        scratch_shapes=[pltpu.VMEM((1024, 128), F32)] * 2,
-    )(info, spread)
+        out_shape=(shape((1024, 128), BF), shape((1024, 128), BF), shape((4, 256, 256), BF)),
+        in_specs=[SMEM, VMEM, HBM],
+        out_specs=(VMEM, VMEM, VMEM),
+        scratch_shapes=[pltpu.VMEM((1024, 128), F32)] * 2 + [pltpu.SemaphoreType.DMA],
+    )(info, spread, in_hbm(t["w"]))
     key_shards = block_gather("k", kn)
 
     gated, ss = kernel(
         conv_kernel,
         "conv",
         out_shape=(shape((32, 16, 256), BF), shape((32, 256), F32)),
-        in_specs=[SMEM, VMEM, SMEM] + [VMEM] * 6 + [HBM],
+        in_specs=[SMEM, VMEM, SMEM] + [VMEM] * 7,
         out_specs=(VMEM, VMEM),
         scratch_shapes=[pltpu.VMEM((2, 512, 128), F32)] * 2
-        + [pltpu.VMEM((512, 256), F32)] * 2
-        + [pltpu.VMEM((4, 256, 256), BF), pltpu.SemaphoreType.DMA],
-    )(info, spread, skip_weight, hr, hi, f1, f2, tc, ts, in_hbm(t["w"]))
+        + [pltpu.VMEM((512, 256), F32)] * 2,
+    )(info, spread, skip_weight, hr, hi, f1, f2, tc, ts, w)
     value_shards = block_gather("v", gated)
 
     keys = kernel(

time: 146 us -> 143 us (0.979)
  the two profiles are of different devices: /device:TPU:32 before, /device:TPU:4 now
where the time goes in v2:
time: 143 us
  waiting for transfers between devices  53 us (37%)
  starting transfers between devices  42.9 us (30%)
  Pallas kernels  25.9 us (18%)
  blocking collectives  19.4 us (14%)
    all_to_all x1, waiting for transfers between devices, local(): spread = lax.all_to_all(packed, 'seq', 0, 0, tiled=True)  24.6 us
    all_to_all x1, blocking collectives, local(): back = lax.all_to_all(back, 'seq', 0, 0, tiled=True)  19.4 us
    ppermute x11, starting transfers between devices, all_sum(): lax.ppermute(x, axis, [(d, d ^ f) for d in range(size)])  15.3 us
    ppermute x11, waiting for transfers between devices, all_sum(): lax.ppermute(x, axis, [(d, d ^ f) for d in range(size)])  15.3 us
    all_to_all x1, starting transfers between devices, local(): spread = lax.all_to_all(packed, 'seq', 0, 0, tiled=True)  11.5 us
    pallas_call x4, Pallas kernels, local(): kernel(functools.partial(score_kernel, tiles), 'score%d' % n, out_shape=(...  8.73 us
    ppermute x2, starting transfers between devices, block_gather(): right = lax.ppermute(own, 'seq', down)  6.63 us
    ppermute x2, waiting for transfers between devices, block_gather(): left = lax.ppermute(own, 'seq', up)  5.89 us
  transfers between devices with their start and end apart: 26, of which 13 were waited for; matrix products, arithmetic and copies ran while one was open for 0% of the time, Pallas kernels for 8%

profile of v2, /device:TPU:4, one launch (start us, length us, event | category | flops | bytes accessed | tf_op | source)
XLA Modules:
  0.0 142.9 jit_solution(5551002380770797598)
XLA Ops:
  0.7 2.6 %shard_map.149 = bf16[32,128,128]{2,1,0:T(8,128)(2,1)} custom-call(bf16[512,256]{1,0:T(8,128)(2,1)} %hk.1, bf16[512,256]{1,0:T(8,128)(2,1)} %hv.1, bf16[512,256]{1,0:T(8,128)(2,1)} %hq.1, bf16[256,512]{1,0:T(8,128)(2,1)} %q.1, bf16[256,512]{1,0:T(8,128)(2,1)} %k.1), custom_call_target="tpu_custom_call" | custom-call | tf_op jit(solution)/shard_map/pallas_call | solution.py:398
  3.2 11.5 %all-to-all-start = ((bf16[32,128,128]{2,1,0:T(8,128)(2,1)}), bf16[32,128,128]{2,1,0:T(8,128)(2,1)S(1)}, u32[]{:S(2)}, u32[]{:S(2)}) async-start(bf16[32,128,128]{2,1,0:T(8,128)(2,1)} %shard_map.149), calls=%async_computation | async-start | bytes 2097152 | tf_op jit(solution)/shard_map/all_to_all | solution.py:408
  15.1 0.2 copy.20
  15.6 2.6 %shard_map.150 = (f32[512,256]{1,0:T(8,128)S(1)}, f32[512,256]{1,0:T(8,128)S(1)}, bf16[128,32]{1,0:T(8,128)(2,1)S(1)}, bf16[64,64]{1,0:T(8,128)(2,1)S(1)}, f32[32,256]{1,0:T(8,128)S(1)}, /*index=5*/f32[32,256]{1,0:T(8,128)S(1)}) custom-call(f32[16,32,256]{2,1,0:T(8,128)S(1)} %bitcast.12, bf16[128,32]{1,0:T(8,128)(2,1)} %constant.104.clone.f1h, ...), custom_call_target="tpu_custom_call" | custom-call | tf_op jit(solution)/shard_map/pallas_call | solution.py:414
  18.2 24.6 %all-to-all-done.x = bf16[32,128,128]{2,1,0:T(8,128)(2,1)S(1)} async-done(((bf16[32,128,128]{2,1,0:T(8,128)(2,1)}), bf16[32,128,128]{2,1,0:T(8,128)(2,1)S(1)}, u32[]{:S(2)}, u32[]{:S(2)}) %all-to-all-start) | async-done | bytes 1048608 | tf_op jit(solution)/shard_map/all_to_all | solution.py:408
  42.8 1.6 %shard_map.151 = (bf16[1024,128]{1,0:T(8,128)(2,1)S(1)}, bf16[1024,128]{1,0:T(8,128)(2,1)S(1)}, bf16[4,256,256]{2,1,0:T(8,128)(2,1)S(1)}) custom-call(s32[72]{0:T(128)S(1)} %concatenate.3.info, bf16[32,128,128]{2,1,0:T(8,128)(2,1)S(1)} %all-to-all-done.x, bf16[4,256,256]{2,1,0:T(8,128)(2,1)} %constant.108.clone.wh), custom_call_target="tpu_custom_call" | custom-call | tf_op jit(solution)/shard_map/pallas_call | solution.py:427
  44.4 4.3 %shard_map.152 = (bf16[32,16,256]{2,1,0:T(8,128)(2,1)S(1)}, f32[32,256]{1,0:T(8,128)S(1)}) custom-call(s32[72]{0:T(128)S(1)} %concatenate.3.info, bf16[32,128,128]{2,1,0:T(8,128)(2,1)S(1)} %all-to-all-done.x, f32[16]{0:T(128)S(1)} %copy-done.1, f32[512,256]{1,0:T(8,128)S(1)} %get-tuple-element.33.hr, f32[512,256]{1,0:T(8,128)S(1)} %get-tuple-element.34.hi, ...), custom_call_target="tpu_custom_call" | custom-call | tf_op jit(solution)/shard_map/pallas_call | solution.py:437
  48.8 1.2 collective-permute-done
  50.0 0.5 collective-permute-start.3
  50.5 2.7 %collective-permute-start.2 = (f32[32,256]{1,0:T(8,128)S(1)}, f32[32,256]{1,0:T(8,128)S(1)}, u32[]{:S(2)}, u32[]{:S(2)}) collective-permute-start(f32[32,256]{1,0:T(8,128)S(1)} %add.144), channel_id=1, source_target_pairs={{0,4},{1,5},{2,6},{3,7},{4,0},{5,1},{6,2},{7,3},{8,12},{9,13},{10,... | collective-permute-start | bytes 98312 | tf_op jit(solution)/shard_map/ppermute | solution.py:345
  53.3 0.8 collective-permute-start.1
  54.1 1.9 %collective-permute-done.2 = f32[32,256]{1,0:T(8,128)S(1)} collective-permute-done((f32[32,256]{1,0:T(8,128)S(1)}, f32[32,256]{1,0:T(8,128)S(1)}, u32[]{:S(2)}, u32[]{:S(2)}) %collective-permute-start.2) | collective-permute-done | bytes 32800 | tf_op jit(solution)/shard_map/ppermute | solution.py:345
  56.0 1.2 collective-permute-done.1
  57.2 1.0 collective-permute-start.6
  58.2 5.5 %collective-permute-start.5 = (f32[32,256]{1,0:T(8,128)S(1)}, f32[32,256]{1,0:T(8,128)S(1)}, u32[]{:S(2)}, u32[]{:S(2)}) collective-permute-start(f32[32,256]{1,0:T(8,128)S(1)} %add_add_fusion.2), channel_id=1, source_target_pairs={{0,128},{8,136},{16,144},{24,152},{32,160},{40,168},{48,176},{56,1... | collective-permute-start | bytes 98312 | tf_op jit(solution)/shard_map/ppermute | solution.py:345
  63.8 2.8 %collective-permute-done.5 = f32[32,256]{1,0:T(8,128)S(1)} collective-permute-done((f32[32,256]{1,0:T(8,128)S(1)}, f32[32,256]{1,0:T(8,128)S(1)}, u32[]{:S(2)}, u32[]{:S(2)}) %collective-permute-start.5) | collective-permute-done | bytes 32800 | tf_op jit(solution)/shard_map/ppermute | solution.py:345
  66.6 1.9 %collective-permute-done.4 = f32[32,256]{1,0:T(8,128)S(1)} collective-permute-done((f32[32,256]{1,0:T(8,128)S(1)}, f32[32,256]{1,0:T(8,128)S(1)}, u32[]{:S(2)}, u32[]{:S(2)}) %collective-permute-start.4) | collective-permute-done | bytes 32800 | tf_op jit(solution)/shard_map/ppermute | solution.py:345
  68.5 1.1 collective-permute-start.9
  69.6 0.8 collective-permute-start.8
  70.4 2.2 %collective-permute-start.7 = (f32[32,256]{1,0:T(8,128)S(1)}, f32[32,256]{1,0:T(8,128)S(1)}, u32[]{:S(2)}, u32[]{:S(2)}) collective-permute-start(f32[32,256]{1,0:T(8,128)S(1)} %add_add_fusion.1), channel_id=1, source_target_pairs={{0,8},{8,0},{16,24},{24,16},{32,40},{40,32},{48,56},{56,48},{64,72... | collective-permute-start | bytes 98312 | tf_op jit(solution)/shard_map/ppermute | solution.py:345
  72.8 1.3 collective-permute-done.9
  74.0 0.7 collective-permute-start.21
  74.7 0.6 collective-permute-done.8
  75.4 0.6 collective-permute-start.11
  76.0 0.4 collective-permute-start.10
  76.4 5.9 %collective-permute-done.18.rest_1_ = bf16[1024,128]{1,0:T(8,128)(2,1)S(1)} collective-permute-done((bf16[1024,128]{1,0:T(8,128)(2,1)S(1)}, bf16[1024,128]{1,0:T(8,128)(2,1)S(1)}, u32[]{:S(2)}, u32[]{:S(2)}) %collective-permute-start.18) | collective-permute-done | bytes 262176 | tf_op jit(solution)/shard_map/ppermute | solution.py:322
  82.3 4.4 %collective-permute-done.10 = f32[32,256]{1,0:T(8,128)S(1)} collective-permute-done((f32[32,256]{1,0:T(8,128)S(1)}, f32[32,256]{1,0:T(8,128)S(1)}, u32[]{:S(2)}, u32[]{:S(2)}) %collective-permute-start.10) | collective-permute-done | bytes 32800 | tf_op jit(solution)/shard_map/ppermute | solution.py:345
  86.7 2.9 %collective-permute-start.19 = (bf16[1024,128]{1,0:T(8,128)(2,1)S(1)}, bf16[1024,128]{1,0:T(8,128)(2,1)S(1)}, u32[]{:S(2)}, u32[]{:S(2)}) collective-permute-start(bf16[1024,128]{1,0:T(8,128)(2,1)S(1)} %get-tuple-element.47.rest_0_), channel_id=1, source_target_pairs={{0,24},{8,0},{16,8},{24,16},{32,56},{40,32},{48,40},{56,48},{64,88... | collective-permute-start | bytes 786440 | tf_op jit(solution)/shard_map/ppermute | solution.py:323
  89.6 0.2 collective-permute-start.16
  89.8 1.0 collective-permute-start.23
  90.8 1.1 collective-permute-start.20
  91.8 1.8 %collective-permute-start.24 = (bf16[1024,128]{1,0:T(8,128)(2,1)S(1)}, bf16[1024,128]{1,0:T(8,128)(2,1)S(1)}, u32[]{:S(2)}, u32[]{:S(2)}) collective-permute-start(bf16[1024,128]{1,0:T(8,128)(2,1)S(1)} %collective-permute-done.22.rest_5_), channel_id=1, source_target_pairs={{0,8},{8,16},{16,24},{24,0},{32,40},{40,48},{48,56},{56,32},{64,72... | collective-permute-start | bytes 786440 | tf_op jit(solution)/shard_map/ppermute | solution.py:329
  93.7 2.6 %collective-permute-done.19.rest_2_ = bf16[1024,128]{1,0:T(8,128)(2,1)S(1)} collective-permute-done((bf16[1024,128]{1,0:T(8,128)(2,1)S(1)}, bf16[1024,128]{1,0:T(8,128)(2,1)S(1)}, u32[]{:S(2)}, u32[]{:S(2)}) %collective-permute-start.19) | collective-permute-done | bytes 262176 | tf_op jit(solution)/shard_map/ppermute | solution.py:323
  96.3 3.7 %collective-permute-start.12 = (bf16[32,16,256]{2,1,0:T(8,128)(2,1)S(1)}, bf16[32,16,256]{2,1,0:T(8,128)(2,1)S(1)}, u32[]{:S(2)}, u32[]{:S(2)}) collective-permute-start(bf16[32,16,256]{2,1,0:T(8,128)(2,1)S(1)} %get-tuple-element.42.rest_0_), channel_id=1, source_target_pairs={{0,24},{8,0},{16,8},{24,16},{32,56},{40,32},{48,40},{56,48},{64,88... | collective-permute-start | bytes 786440 | tf_op jit(solution)/shard_map/ppermute | solution.py:323
  100.0 1.9 %collective-permute-done.16.rest_6_ = bf16[32,16,256]{2,1,0:T(8,128)(2,1)S(1)} collective-permute-done((bf16[32,16,256]{2,1,0:T(8,128)(2,1)S(1)}, bf16[32,16,256]{2,1,0:T(8,128)(2,1)S(1)}, u32[]{:S(2)}, u32[]{:S(2)}) %collective-permute-start.16) | collective-permute-done | bytes 262176 | tf_op jit(solution)/shard_map/ppermute | solution.py:327
  101.9 0.3 collective-permute-start.15
  102.2 2.7 %collective-permute-done.23.rest_6_ = bf16[1024,128]{1,0:T(8,128)(2,1)S(1)} collective-permute-done((bf16[1024,128]{1,0:T(8,128)(2,1)S(1)}, bf16[1024,128]{1,0:T(8,128)(2,1)S(1)}, u32[]{:S(2)}, u32[]{:S(2)}) %collective-permute-start.23) | collective-permute-done | bytes 262176 | tf_op jit(solution)/shard_map/ppermute | solution.py:327
  104.9 1.5 %collective-permute-start.13 = (bf16[32,16,256]{2,1,0:T(8,128)(2,1)S(1)}, bf16[32,16,256]{2,1,0:T(8,128)(2,1)S(1)}, u32[]{:S(2)}, u32[]{:S(2)}) collective-permute-start(bf16[32,16,256]{2,1,0:T(8,128)(2,1)S(1)} %collective-permute-done.11.rest_1_), channel_id=1, source_target_pairs={{0,8},{8,16},{16,24},{24,0},{32,40},{40,48},{48,56},{56,32},{64,72... | collective-permute-start | bytes 786440 | tf_op jit(solution)/shard_map/ppermute | solution.py:325
  106.4 2.2 %collective-permute-start.17 = (bf16[32,16,256]{2,1,0:T(8,128)(2,1)S(1)}, bf16[32,16,256]{2,1,0:T(8,128)(2,1)S(1)}, u32[]{:S(2)}, u32[]{:S(2)}) collective-permute-start(bf16[32,16,256]{2,1,0:T(8,128)(2,1)S(1)} %collective-permute-done.16.rest_6_), channel_id=1, source_target_pairs={{0,24},{8,0},{16,8},{24,16},{32,56},{40,32},{48,40},{56,48},{64,88... | collective-permute-start | bytes 786440 | tf_op jit(solution)/shard_map/ppermute | solution.py:331
  108.6 0.8 shard_map.154.keys
  109.4 2.0 %shard_map.156 = (bf16[128,7168]{1,0:T(8,128)(2,1)S(1)}, f32[128,1]{1,0:T(8,128)S(1)}) custom-call(s32[128,1]{1,0:T(8,128)S(1)} %fusion.2.qloc, bf16[1024,128]{1,0:T(8,128)(2,1)S(1)} %get-tuple-element.46.q, bf16[8,1024,128]{2,1,0:T(8,128)(2,1)S(1)} %shard_map.154.keys), custom_call_target="tpu_custom_call" | custom-call | tf_op jit(solution)/shard_map/pallas_call | solution.py:460
  111.4 2.1 %shard_map.155 = (bf16[128,8192]{1,0:T(8,128)(2,1)S(1)}, f32[128,1]{1,0:T(8,128)S(1)}) custom-call(s32[128,1]{1,0:T(8,128)S(1)} %fusion.2.qloc, bf16[1024,128]{1,0:T(8,128)(2,1)S(1)} %get-tuple-element.46.q, bf16[8,1024,128]{2,1,0:T(8,128)(2,1)S(1)} %shard_map.154.keys), custom_call_target="tpu_custom_call" | custom-call | tf_op jit(solution)/shard_map/pallas_call | solution.py:460
  113.5 3.1 %shard_map.157 = (bf16[256,6144]{1,0:T(8,128)(2,1)S(1)}, f32[256,1]{1,0:T(8,128)S(1)}) custom-call(s32[128,1]{1,0:T(8,128)S(1)} %fusion.2.qloc, bf16[1024,128]{1,0:T(8,128)(2,1)S(1)} %get-tuple-element.46.q, bf16[8,1024,128]{2,1,0:T(8,128)(2,1)S(1)} %shard_map.154.keys), custom_call_target="tpu_custom_call" | custom-call | tf_op jit(solution)/shard_map/pallas_call | solution.py:460
  116.6 1.5 %shard_map.158 = (bf16[512,4096]{1,0:T(8,128)(2,1)S(1)}, f32[512,1]{1,0:T(8,128)S(1)}) custom-call(s32[128,1]{1,0:T(8,128)S(1)} %fusion.2.qloc, bf16[1024,128]{1,0:T(8,128)(2,1)S(1)} %get-tuple-element.46.q, bf16[8,1024,128]{2,1,0:T(8,128)(2,1)S(1)} %shard_map.154.keys), custom_call_target="tpu_custom_call" | custom-call | tf_op jit(solution)/shard_map/pallas_call | solution.py:460
  118.2 1.5 %shard_map.153 = (bf16[32,128,256]{2,1,0:T(8,128)(2,1)S(1)}, bf16[32,32,128]{2,1,0:T(8,128)(2,1)S(1)}) custom-call(s32[72]{0:T(128)S(1)} %concatenate.3.info, bf16[32,16,256]{2,1,0:T(8,128)(2,1)S(1)} %get-tuple-element.42.rest_0_, bf16[32,16,256]{2,1,0:T(8,128)(2,1)S(1)} %collective-permute-done.11.rest_1_, ...), custom_call_target="tpu_custom_call" | custom-call | tf_op jit(solution)/shard_map/pallas_call | solution.py:471
  119.6 2.9 %shard_map.159 = bf16[32,64,128]{2,1,0:T(8,128)(2,1)S(1)} custom-call(f32[32,256]{1,0:T(8,128)S(1)} %add.154.ss, f32[1,128]{1,0:T(1,128)S(1)} %dynamic-slice_bitcast_fusion.gain, bf16[32,128,256]{2,1,0:T(8,128)(2,1)S(1)} %get-tuple-element.43.vals, bf16[32,32,128]{2,1,0:T(8,128)(2,1)S(1)} %get-tuple-element.44.hyena, ...), custom_call_target="tpu_custom_call" | custom-call | tf_op jit(solution)/shard_map/pallas_call | solution.py:480
  122.5 19.4 %all_to_all.10.x = bf16[32,64,128]{2,1,0:T(8,128)(2,1)S(1)} all-to-all(bf16[32,64,128]{2,1,0:T(8,128)(2,1)S(1)} %shard_map.159), channel_id=1, replica_groups=mesh['seq'=32,'chan'=8] {'seq'}, dimensions={0} | all-to-all | bytes 1048576 | tf_op jit(solution)/shard_map/all_to_all | solution.py:492
  141.9 1.0 shard_map.160
  (39 shorter events, 1.0 us)
Async XLA Ops:
  0.6 14.9 %copy-start = (f32[512]{0:T(512)S(1)}, f32[512]{0:T(512)}, u32[]{:S(2)}) copy-start(f32[512]{0:T(512)} %param.22) | copy-start | bytes 6148
  0.6 14.2 %copy-start.3 = (s32[8192]{0:T(1024)S(1)}, s32[8192]{0:T(1024)}, u32[]{:S(2)}) copy-start(s32[8192]{0:T(1024)} %param.19) | copy-start | bytes 98308
  0.7 14.5 %copy-start.2 = (f32[16,8192]{1,0:T(8,128)S(1)}, f32[16,8192]{1,0:T(8,128)}, u32[]{:S(2)}) copy-start(f32[16,8192]{1,0:T(8,128)} %param.17) | copy-start | bytes 1572868
  3.2 39.6 %all-to-all-start = ((bf16[32,128,128]{2,1,0:T(8,128)(2,1)}), bf16[32,128,128]{2,1,0:T(8,128)(2,1)S(1)}, u32[]{:S(2)}, u32[]{:S(2)}) async-start(bf16[32,128,128]{2,1,0:T(8,128)(2,1)} %shard_map.149), calls=%async_computation | async-start | bytes 2097152 | tf_op jit(solution)/shard_map/all_to_all | solution.py:408
  14.8 29.6 %copy-start.1 = (f32[16]{0:T(128)S(1)}, f32[16]{0:T(128)}, u32[]{:S(2)}) copy-start(f32[16]{0:T(128)} %skip.1) | copy-start | bytes 196
  48.7 1.3 collective-permute-start
  50.0 4.1 %collective-permute-start.3 = (f32[32,256]{1,0:T(8,128)S(1)}, f32[32,256]{1,0:T(8,128)S(1)}, u32[]{:S(2)}, u32[]{:S(2)}) collective-permute-start(f32[32,256]{1,0:T(8,128)S(1)} %add.144), channel_id=1, source_target_pairs={{0,6},{1,7},{2,4},{3,5},{4,2},{5,3},{6,0},{7,1},{8,14},{9,15},{10,... | collective-permute-start | bytes 98312 | tf_op jit(solution)/shard_map/ppermute | solution.py:345
  50.5 5.4 %collective-permute-start.2 = (f32[32,256]{1,0:T(8,128)S(1)}, f32[32,256]{1,0:T(8,128)S(1)}, u32[]{:S(2)}, u32[]{:S(2)}) collective-permute-start(f32[32,256]{1,0:T(8,128)S(1)} %add.144), channel_id=1, source_target_pairs={{0,4},{1,5},{2,6},{3,7},{4,0},{5,1},{6,2},{7,3},{8,12},{9,13},{10,... | collective-permute-start | bytes 98312 | tf_op jit(solution)/shard_map/ppermute | solution.py:345
  53.3 3.9 %collective-permute-start.1 = (f32[32,256]{1,0:T(8,128)S(1)}, f32[32,256]{1,0:T(8,128)S(1)}, u32[]{:S(2)}, u32[]{:S(2)}) collective-permute-start(f32[32,256]{1,0:T(8,128)S(1)} %add.144), channel_id=1, source_target_pairs={{0,2},{1,3},{2,0},{3,1},{4,6},{5,7},{6,4},{7,5},{8,10},{9,11},{10,... | collective-permute-start | bytes 98312 | tf_op jit(solution)/shard_map/ppermute | solution.py:345
  57.2 6.6 %collective-permute-start.6 = (f32[32,256]{1,0:T(8,128)S(1)}, f32[32,256]{1,0:T(8,128)S(1)}, u32[]{:S(2)}, u32[]{:S(2)}) collective-permute-start(f32[32,256]{1,0:T(8,128)S(1)} %add_add_fusion.2), channel_id=1, source_target_pairs={{0,192},{8,200},{16,208},{24,216},{32,224},{40,232},{48,240},{56,2... | collective-permute-start | bytes 98312 | tf_op jit(solution)/shard_map/ppermute | solution.py:345
  58.2 8.4 %collective-permute-start.5 = (f32[32,256]{1,0:T(8,128)S(1)}, f32[32,256]{1,0:T(8,128)S(1)}, u32[]{:S(2)}, u32[]{:S(2)}) collective-permute-start(f32[32,256]{1,0:T(8,128)S(1)} %add_add_fusion.2), channel_id=1, source_target_pairs={{0,128},{8,136},{16,144},{24,152},{32,160},{40,168},{48,176},{56,1... | collective-permute-start | bytes 98312 | tf_op jit(solution)/shard_map/ppermute | solution.py:345
  63.6 4.8 %collective-permute-start.4 = (f32[32,256]{1,0:T(8,128)S(1)}, f32[32,256]{1,0:T(8,128)S(1)}, u32[]{:S(2)}, u32[]{:S(2)}) collective-permute-start(f32[32,256]{1,0:T(8,128)S(1)} %add_add_fusion.2), channel_id=1, source_target_pairs={{0,64},{8,72},{16,80},{24,88},{32,96},{40,104},{48,112},{56,120},{... | collective-permute-start | bytes 98312 | tf_op jit(solution)/shard_map/ppermute | solution.py:345
  68.5 5.6 %collective-permute-start.9 = (f32[32,256]{1,0:T(8,128)S(1)}, f32[32,256]{1,0:T(8,128)S(1)}, u32[]{:S(2)}, u32[]{:S(2)}) collective-permute-start(f32[32,256]{1,0:T(8,128)S(1)} %add_add_fusion.1), channel_id=1, source_target_pairs={{0,24},{8,16},{16,8},{24,0},{32,56},{40,48},{48,40},{56,32},{64,88... | collective-permute-start | bytes 98312 | tf_op jit(solution)/shard_map/ppermute | solution.py:345
  69.6 5.8 %collective-permute-start.8 = (f32[32,256]{1,0:T(8,128)S(1)}, f32[32,256]{1,0:T(8,128)S(1)}, u32[]{:S(2)}, u32[]{:S(2)}) collective-permute-start(f32[32,256]{1,0:T(8,128)S(1)} %add_add_fusion.1), channel_id=1, source_target_pairs={{0,16},{8,24},{16,0},{24,8},{32,48},{40,56},{48,32},{56,40},{64,80... | collective-permute-start | bytes 98312 | tf_op jit(solution)/shard_map/ppermute | solution.py:345
  70.4 5.5 %collective-permute-start.7 = (f32[32,256]{1,0:T(8,128)S(1)}, f32[32,256]{1,0:T(8,128)S(1)}, u32[]{:S(2)}, u32[]{:S(2)}) collective-permute-start(f32[32,256]{1,0:T(8,128)S(1)} %add_add_fusion.1), channel_id=1, source_target_pairs={{0,8},{8,0},{16,24},{24,16},{32,40},{40,32},{48,56},{56,48},{64,72... | collective-permute-start | bytes 98312 | tf_op jit(solution)/shard_map/ppermute | solution.py:345
  72.7 9.6 %collective-permute-start.18 = (bf16[1024,128]{1,0:T(8,128)(2,1)S(1)}, bf16[1024,128]{1,0:T(8,128)(2,1)S(1)}, u32[]{:S(2)}, u32[]{:S(2)}) collective-permute-start(bf16[1024,128]{1,0:T(8,128)(2,1)S(1)} %get-tuple-element.47.rest_0_), channel_id=1, source_target_pairs={{0,8},{8,16},{16,24},{24,0},{32,40},{40,48},{48,56},{56,32},{64,72... | collective-permute-start | bytes 786440 | tf_op jit(solution)/shard_map/ppermute | solution.py:322
  72.7 16.9 %collective-permute-start.14 = (bf16[32,16,256]{2,1,0:T(8,128)(2,1)S(1)}, bf16[32,16,256]{2,1,0:T(8,128)(2,1)S(1)}, u32[]{:S(2)}, u32[]{:S(2)}) collective-permute-start(bf16[32,16,256]{2,1,0:T(8,128)(2,1)S(1)} %get-tuple-element.42.rest_0_), channel_id=1, source_target_pairs={{0,32},{8,40},{16,48},{24,56},{32,0},{40,8},{48,16},{56,24},{64,96... | collective-permute-start | bytes 786440 | tf_op jit(solution)/shard_map/ppermute | solution.py:324
  74.0 15.8 %collective-permute-start.21 = (bf16[1024,128]{1,0:T(8,128)(2,1)S(1)}, bf16[1024,128]{1,0:T(8,128)(2,1)S(1)}, u32[]{:S(2)}, u32[]{:S(2)}) collective-permute-start(bf16[1024,128]{1,0:T(8,128)(2,1)S(1)} %get-tuple-element.47.rest_0_), channel_id=1, source_target_pairs={{0,32},{8,40},{16,48},{24,56},{32,0},{40,8},{48,16},{56,24},{64,96... | collective-permute-start | bytes 786440 | tf_op jit(solution)/shard_map/ppermute | solution.py:324
  75.4 15.4 %collective-permute-start.11 = (bf16[32,16,256]{2,1,0:T(8,128)(2,1)S(1)}, bf16[32,16,256]{2,1,0:T(8,128)(2,1)S(1)}, u32[]{:S(2)}, u32[]{:S(2)}) collective-permute-start(bf16[32,16,256]{2,1,0:T(8,128)(2,1)S(1)} %get-tuple-element.42.rest_0_), channel_id=1, source_target_pairs={{0,8},{8,16},{16,24},{24,0},{32,40},{40,48},{48,56},{56,32},{64,72... | collective-permute-start | bytes 786440 | tf_op jit(solution)/shard_map/ppermute | solution.py:322
  76.0 10.7 %collective-permute-start.10 = (f32[32,256]{1,0:T(8,128)S(1)}, f32[32,256]{1,0:T(8,128)S(1)}, u32[]{:S(2)}, u32[]{:S(2)}) collective-permute-start(f32[32,256]{1,0:T(8,128)S(1)} %add_add_fusion), channel_id=1, source_target_pairs={{0,32},{8,40},{16,48},{24,56},{32,0},{40,8},{48,16},{56,24},{64,96... | collective-permute-start | bytes 98312 | tf_op jit(solution)/shard_map/ppermute | solution.py:345
  82.2 9.6 %collective-permute-start.22 = (bf16[1024,128]{1,0:T(8,128)(2,1)S(1)}, bf16[1024,128]{1,0:T(8,128)(2,1)S(1)}, u32[]{:S(2)}, u32[]{:S(2)}) collective-permute-start(bf16[1024,128]{1,0:T(8,128)(2,1)S(1)} %collective-permute-done.18.rest_1_), channel_id=1, source_target_pairs={{0,32},{8,40},{16,48},{24,56},{32,0},{40,8},{48,16},{56,24},{64,96... | collective-permute-start | bytes 786440 | tf_op jit(solution)/shard_map/ppermute | solution.py:326
  86.7 9.6 %collective-permute-start.19 = (bf16[1024,128]{1,0:T(8,128)(2,1)S(1)}, bf16[1024,128]{1,0:T(8,128)(2,1)S(1)}, u32[]{:S(2)}, u32[]{:S(2)}) collective-permute-start(bf16[1024,128]{1,0:T(8,128)(2,1)S(1)} %get-tuple-element.47.rest_0_), channel_id=1, source_target_pairs={{0,24},{8,0},{16,8},{24,16},{32,56},{40,32},{48,40},{56,48},{64,88... | collective-permute-start | bytes 786440 | tf_op jit(solution)/shard_map/ppermute | solution.py:323
  89.6 12.3 %collective-permute-start.16 = (bf16[32,16,256]{2,1,0:T(8,128)(2,1)S(1)}, bf16[32,16,256]{2,1,0:T(8,128)(2,1)S(1)}, u32[]{:S(2)}, u32[]{:S(2)}) collective-permute-start(bf16[32,16,256]{2,1,0:T(8,128)(2,1)S(1)} %collective-permute-done.14.rest_4_), channel_id=1, source_target_pairs={{0,24},{8,0},{16,8},{24,16},{32,56},{40,32},{48,40},{56,48},{64,88... | collective-permute-start | bytes 786440 | tf_op jit(solution)/shard_map/ppermute | solution.py:327
  89.8 15.1 %collective-permute-start.23 = (bf16[1024,128]{1,0:T(8,128)(2,1)S(1)}, bf16[1024,128]{1,0:T(8,128)(2,1)S(1)}, u32[]{:S(2)}, u32[]{:S(2)}) collective-permute-start(bf16[1024,128]{1,0:T(8,128)(2,1)S(1)} %collective-permute-done.21.rest_4_), channel_id=1, source_target_pairs={{0,24},{8,0},{16,8},{24,16},{32,56},{40,32},{48,40},{56,48},{64,88... | collective-permute-start | bytes 786440 | tf_op jit(solution)/shard_map/ppermute | solution.py:327
  90.8 15.6 %collective-permute-start.20 = (bf16[1024,128]{1,0:T(8,128)(2,1)S(1)}, bf16[1024,128]{1,0:T(8,128)(2,1)S(1)}, u32[]{:S(2)}, u32[]{:S(2)}) collective-permute-start(bf16[1024,128]{1,0:T(8,128)(2,1)S(1)} %collective-permute-done.18.rest_1_), channel_id=1, source_target_pairs={{0,8},{8,16},{16,24},{24,0},{32,40},{40,48},{48,56},{56,32},{64,72... | collective-permute-start | bytes 786440 | tf_op jit(solution)/shard_map/ppermute | solution.py:325
  91.8 16.8 %collective-permute-start.24 = (bf16[1024,128]{1,0:T(8,128)(2,1)S(1)}, bf16[1024,128]{1,0:T(8,128)(2,1)S(1)}, u32[]{:S(2)}, u32[]{:S(2)}) collective-permute-start(bf16[1024,128]{1,0:T(8,128)(2,1)S(1)} %collective-permute-done.22.rest_5_), channel_id=1, source_target_pairs={{0,8},{8,16},{16,24},{24,0},{32,40},{40,48},{48,56},{56,32},{64,72... | collective-permute-start | bytes 786440 | tf_op jit(solution)/shard_map/ppermute | solution.py:329
  96.3 21.8 %collective-permute-start.12 = (bf16[32,16,256]{2,1,0:T(8,128)(2,1)S(1)}, bf16[32,16,256]{2,1,0:T(8,128)(2,1)S(1)}, u32[]{:S(2)}, u32[]{:S(2)}) collective-permute-start(bf16[32,16,256]{2,1,0:T(8,128)(2,1)S(1)} %get-tuple-element.42.rest_0_), channel_id=1, source_target_pairs={{0,24},{8,0},{16,8},{24,16},{32,56},{40,32},{48,40},{56,48},{64,88... | collective-permute-start | bytes 786440 | tf_op jit(solution)/shard_map/ppermute | solution.py:323
  101.9 16.2 %collective-permute-start.15 = (bf16[32,16,256]{2,1,0:T(8,128)(2,1)S(1)}, bf16[32,16,256]{2,1,0:T(8,128)(2,1)S(1)}, u32[]{:S(2)}, u32[]{:S(2)}) collective-permute-start(bf16[32,16,256]{2,1,0:T(8,128)(2,1)S(1)} %collective-permute-done.11.rest_1_), channel_id=1, source_target_pairs={{0,32},{8,40},{16,48},{24,56},{32,0},{40,8},{48,16},{56,24},{64,96... | collective-permute-start | bytes 786440 | tf_op jit(solution)/shard_map/ppermute | solution.py:326
  104.9 13.2 %collective-permute-start.13 = (bf16[32,16,256]{2,1,0:T(8,128)(2,1)S(1)}, bf16[32,16,256]{2,1,0:T(8,128)(2,1)S(1)}, u32[]{:S(2)}, u32[]{:S(2)}) collective-permute-start(bf16[32,16,256]{2,1,0:T(8,128)(2,1)S(1)} %collective-permute-done.11.rest_1_), channel_id=1, source_target_pairs={{0,8},{8,16},{16,24},{24,0},{32,40},{40,48},{48,56},{56,32},{64,72... | collective-permute-start | bytes 786440 | tf_op jit(solution)/shard_map/ppermute | solution.py:325
  106.4 11.8 %collective-permute-start.17 = (bf16[32,16,256]{2,1,0:T(8,128)(2,1)S(1)}, bf16[32,16,256]{2,1,0:T(8,128)(2,1)S(1)}, u32[]{:S(2)}, u32[]{:S(2)}) collective-permute-start(bf16[32,16,256]{2,1,0:T(8,128)(2,1)S(1)} %collective-permute-done.16.rest_6_), channel_id=1, source_target_pairs={{0,24},{8,0},{16,8},{24,16},{32,56},{40,32},{48,40},{56,48},{64,88... | collective-permute-start | bytes 786440 | tf_op jit(solution)/shard_map/ppermute | solution.py:331
